TPU v7x, 32 devices: a whole 2x2x4 slice. The times are simulated.
32 devices in a mesh: dp: 8 (over y, x, core), sp: 4 (over z).
Axes of the slice: x: 2, y: 2, z: 4, core: 2. Of those that a mesh axis runs over, the one named last changes fastest.
Arguments:
- tokens: bfloat16 [8192, 2048], P(('dp', 'sp')), may hold values from -6 to 6
- lengths: int32 [8], P('dp'), may hold values from 64 to 1024, as said below
- cotangent: bfloat16 [8192, 2048], P(('dp', 'sp')), may hold values from -6 to 6
- ln_gains: bfloat16 [2, 2048], replicated, may hold values from 0.099609375 to 1.8984375
- ln_shifts: bfloat16 [2, 2048], replicated, may hold values from -1.5 to 1.5
- qkv_weight: bfloat16 [2048, 6144], P(('dp', 'sp')), may hold values from -0.125 to 0.125
- qkv_bias: bfloat16 [3, 2048], replicated, may hold values from -0.25 to 0.25
- out_weight: bfloat16 [2048, 2048], P(('dp', 'sp')), may hold values from -1 to 1
- up_weight: bfloat16 [8192, 2048], P(('dp', 'sp')), may hold values from -0.125 to 0.125
- up_bias: bfloat16 [8192], replicated, may hold values from -1.5 to 1.5
- down_weight: bfloat16 [8192, 2048], P(('dp', 'sp')), may hold values from -0.0625 to 0.0625
- out_bias: bfloat16 [2048], replicated, may hold values from -1.5 to 1.5
Outputs:
- output: bfloat16 [8192, 2048], P(('dp', 'sp'))
- input_grad: bfloat16 [8192, 2048], P(('dp', 'sp'))
- ln_gains_grad: float32 [2, 2048], replicated
- ln_shifts_grad: float32 [2, 2048], replicated
- qkv_weight_grad: float32 [2048, 6144], P(('dp', 'sp'))
- qkv_bias_grad: float32 [3, 2048], replicated
- out_weight_grad: float32 [2048, 2048], P(('dp', 'sp'))
- up_weight_grad: float32 [8192, 2048], P(('dp', 'sp'))
- up_bias_grad: float32 [8192], replicated
- down_weight_grad: float32 [8192, 2048], P(('dp', 'sp'))
- out_bias_grad: float32 [2048], replicated
Inputs may be any that keep to these rules, and one draw needn't show every extreme that they name: `lengths`: a sequence's valid tokens fill the front of its 1024 rows; the first sequence is always full.
All inputs are finite; a program needn't handle non-finite values.
Results may differ from a plain program's by a relative error of at most 0.011.
Values may be sent and summed in bfloat16 or wider, within the bound.
A program may use at most 768 MiB of HBM per device.

v0:
```python
import jax
import jax.numpy as jnp
from jax import lax
from jax.sharding import PartitionSpec as P

D = 2048
HEADS = 8
HEAD = 256
ROT = 64


eps = 1e-05
base_freq = 10000.0
root_half = 0.7071067811865476
inv_root_two_pi = 0.3989422804014327


def contract_rows(left, right):
    return lax.dot_general(
        left, right, (((0,), (0,)), ((), ())), preferred_element_type=jnp.float32
    )


def contract_cols(left, right):
    return lax.dot_general(
        left, right, (((1,), (1,)), ((), ())), preferred_element_type=jnp.float32
    )


def gelu_value(pre_act):
    return 0.5 * pre_act * (1.0 + lax.erf(pre_act * root_half))


def gelu_slope(pre_act):
    return 0.5 * (1.0 + lax.erf(pre_act * root_half)) + pre_act * inv_root_two_pi * jnp.exp(
        -0.5 * pre_act * pre_act
    )


def rotary_tables(positions):
    half_rot = ROT // 2
    frequency = base_freq ** (-jnp.arange(half_rot, dtype=jnp.float32) * (2.0 / ROT))
    angles = positions.astype(jnp.float32)[:, None] * frequency[None, :]
    return (jnp.cos(angles)[:, None, :], jnp.sin(angles)[:, None, :])


def rotate(tensor_in, cosine, sine_table):
    half_rot = cosine.shape[-1]
    leading = tensor_in[..., :half_rot]
    trailing = tensor_in[..., half_rot : 2 * half_rot]
    return jnp.concatenate(
        [
            leading * cosine - trailing * sine_table,
            trailing * cosine + leading * sine_table,
            tensor_in[..., 2 * half_rot :],
        ],
        axis=-1,
    )


def block_mask(block_start, block_rows, seq_len, length):
    key_pos = jnp.arange(seq_len, dtype=jnp.int32)
    query_pos = block_start + jnp.arange(block_rows, dtype=jnp.int32)
    return (key_pos[None, :] <= query_pos[:, None]) & (key_pos[None, :] < length)


def attend_forward(queries, key_rows, values, length, score_scale):
    seq_len, head_width = queries.shape
    head_count = head_width // HEAD
    block_rows = min(512, seq_len)
    key_heads = key_rows.reshape(seq_len, head_count, HEAD)
    value_heads = values.reshape(seq_len, head_count, HEAD)

    def one_block(block_start):
        query_rows = lax.dynamic_slice_in_dim(queries, block_start, block_rows, 0).reshape(
            block_rows, head_count, HEAD
        )
        scores = (
            jnp.einsum("qhd,khd->hqk", query_rows, key_heads, preferred_element_type=jnp.float32)
            * score_scale
        )
        allowed = block_mask(block_start, block_rows, seq_len, length)
        scores = jnp.where(allowed[None], scores, -1e30)
        highest = jnp.max(scores, axis=-1, keepdims=True)
        weights_raw = jnp.exp(scores - highest)
        row_totals = jnp.sum(weights_raw, axis=-1, keepdims=True)
        weights_low = (weights_raw / row_totals).astype(jnp.bfloat16)
        context = jnp.einsum(
            "hqk,khd->qhd", weights_low, value_heads, preferred_element_type=jnp.float32
        )
        return (
            context.reshape(block_rows, head_width).astype(jnp.bfloat16),
            (highest + jnp.log(row_totals))[..., 0],
        )

    starts = jnp.arange(seq_len // block_rows, dtype=jnp.int32) * block_rows
    context, log_sums = lax.map(one_block, starts)
    return (context.reshape(seq_len, head_width), log_sums)


def attend_backward(queries, key_rows, values, grad_context, log_sums, length, score_scale):
    seq_len, head_width = queries.shape
    head_count = head_width // HEAD
    block_rows = min(512, seq_len)
    key_heads = key_rows.reshape(seq_len, head_count, HEAD)
    value_heads = values.reshape(seq_len, head_count, HEAD)

    def one_block(running, entry):
        grad_keys, grad_values = running
        block_start, lse_block = entry
        query_rows = lax.dynamic_slice_in_dim(queries, block_start, block_rows, 0).reshape(
            block_rows, head_count, HEAD
        )
        grad_rows = lax.dynamic_slice_in_dim(grad_context, block_start, block_rows, 0).reshape(
            block_rows, head_count, HEAD
        )
        scores = (
            jnp.einsum("qhd,khd->hqk", query_rows, key_heads, preferred_element_type=jnp.float32)
            * score_scale
        )
        allowed = block_mask(block_start, block_rows, seq_len, length)
        weights_full = jnp.where(allowed[None], jnp.exp(scores - lse_block[..., None]), 0.0)
        grad_values = grad_values + jnp.einsum(
            "hqk,qhd->khd",
            weights_full.astype(jnp.bfloat16),
            grad_rows,
            preferred_element_type=jnp.float32,
        )
        grad_probs = jnp.einsum(
            "qhd,khd->hqk", grad_rows, value_heads, preferred_element_type=jnp.float32
        )
        inner_sum = jnp.sum(weights_full * grad_probs, axis=-1, keepdims=True)
        grad_scores = (weights_full * (grad_probs - inner_sum)).astype(jnp.bfloat16)
        grad_query = (
            jnp.einsum("hqk,khd->qhd", grad_scores, key_heads, preferred_element_type=jnp.float32)
            * score_scale
        )
        grad_keys = (
            grad_keys
            + jnp.einsum(
                "hqk,qhd->khd", grad_scores, query_rows, preferred_element_type=jnp.float32
            )
            * score_scale
        )
        return ((grad_keys, grad_values), grad_query.reshape(block_rows, head_width))

    starts = jnp.arange(seq_len // block_rows, dtype=jnp.int32) * block_rows
    zero_heads = jnp.zeros((seq_len, head_count, HEAD), jnp.float32)
    (grad_keys, grad_values), grad_queries = lax.scan(
        one_block, (zero_heads, zero_heads), (starts, log_sums)
    )
    return (
        grad_queries.reshape(seq_len, head_width),
        grad_keys.reshape(seq_len, head_width),
        grad_values.reshape(seq_len, head_width),
    )


def body(
    tokens,
    lengths,
    cotangent,
    ln_gains,
    ln_shifts,
    qkv_weight,
    qkv_bias,
    out_weight,
    up_weight,
    up_bias,
    down_weight,
    out_bias,
):
    row_count = tokens.shape[0]
    local_rows = qkv_weight.shape[0]
    score_scale = HEAD ** (-0.5)
    length = lengths[0]
    positions = lax.axis_index("sp") * row_count + jnp.arange(row_count, dtype=jnp.int32)
    cosine, sine_table = rotary_tables(positions)
    inputs = tokens.astype(jnp.float32)
    gains = ln_gains.astype(jnp.float32)
    shifts = ln_shifts.astype(jnp.float32)
    centre = jnp.mean(inputs, axis=-1, keepdims=True)
    centered = inputs - centre
    inverse = lax.rsqrt(jnp.mean(centered * centered, axis=-1, keepdims=True) + eps)
    normed = centered * inverse
    attn_in = (normed * gains[0] + shifts[0]).astype(jnp.bfloat16)
    mlp_in = (normed * gains[1] + shifts[1]).astype(jnp.bfloat16)
    unit_bias = up_bias.astype(jnp.float32)
    up_flat = up_weight.reshape(local_rows, 4 * D)
    down_flat = down_weight.reshape(local_rows, 4 * D)
    qkv_piece = lax.all_gather(qkv_weight, ("dp", "sp"), axis=0, tiled=True)
    up_piece = lax.all_gather(up_flat, ("dp", "sp"), axis=0, tiled=True)
    down_piece = lax.all_gather(down_flat, ("dp", "sp"), axis=0, tiled=True)
    piece_rows = qkv_piece.shape[0]
    projected = jnp.dot(attn_in, qkv_piece, preferred_element_type=jnp.float32)
    up_rows = up_piece.reshape(4 * piece_rows, D)
    down_rows = down_piece.reshape(4 * piece_rows, D)
    pre_act = contract_cols(mlp_in, up_rows) + unit_bias
    hidden = gelu_value(pre_act).astype(jnp.bfloat16)
    mlp_out = jnp.dot(hidden, down_rows, preferred_element_type=jnp.float32)
    front_stored = pre_act
    projected, stored, mlp_out = (projected, front_stored, mlp_out)
    projected = projected + qkv_bias.astype(jnp.float32).reshape(3 * D)
    queries = rotate(projected[:, :D].reshape(row_count, HEADS, HEAD), cosine, sine_table).reshape(
        row_count, D
    )
    key_rows = rotate(
        projected[:, D : 2 * D].reshape(row_count, HEADS, HEAD), cosine, sine_table
    ).reshape(row_count, D)
    packed = jnp.stack([queries, key_rows, projected[:, 2 * D :]]).astype(jnp.bfloat16)
    head_major = lax.all_to_all(packed, "sp", split_axis=2, concat_axis=1, tiled=True)
    context_heads, log_sums = attend_forward(
        head_major[0], head_major[1], head_major[2], length, score_scale
    )
    context = lax.all_to_all(context_heads, "sp", split_axis=0, concat_axis=1, tiled=True)
    attn_out = jnp.dot(
        context,
        lax.all_gather(out_weight, ("dp", "sp"), axis=0, tiled=True),
        preferred_element_type=jnp.float32,
    )
    output = (inputs + attn_out + mlp_out + out_bias.astype(jnp.float32)).astype(jnp.bfloat16)
    row_valid = (positions < length).astype(jnp.float32)
    grad_out = (cotangent.astype(jnp.float32) * row_valid[:, None]).astype(jnp.bfloat16)
    out_piece = lax.all_gather(out_weight, ("dp", "sp"), axis=0, tiled=True)
    up_piece = lax.all_gather(up_flat, ("dp", "sp"), axis=0, tiled=True)
    down_piece = lax.all_gather(down_flat, ("dp", "sp"), axis=0, tiled=True)
    piece_rows = out_piece.shape[0]
    grad_context = contract_cols(grad_out, out_piece)
    up_rows = up_piece.reshape(4 * piece_rows, D)
    down_rows = down_piece.reshape(4 * piece_rows, D)
    grad_hidden = contract_cols(grad_out, down_rows)
    pre_act = stored
    grad_low = (grad_hidden * gelu_slope(pre_act)).astype(jnp.bfloat16)
    grad_mlp_in = jnp.dot(grad_low, up_rows, preferred_element_type=jnp.float32)
    grad_context, grad_mlp_in, grad_pre = (grad_context, grad_mlp_in, grad_low)
    grad_heads = lax.all_to_all(
        grad_context.astype(jnp.bfloat16), "sp", split_axis=1, concat_axis=0, tiled=True
    )
    grad_queries, grad_keys, grad_values = attend_backward(
        head_major[0], head_major[1], head_major[2], grad_heads, log_sums, length, score_scale
    )
    grad_packed = jnp.stack([grad_queries, grad_keys, grad_values]).astype(jnp.bfloat16)
    grad_tokens = lax.all_to_all(grad_packed, "sp", split_axis=1, concat_axis=2, tiled=True)
    grad_query_rows = rotate(
        grad_tokens[0].astype(jnp.float32).reshape(row_count, HEADS, HEAD), cosine, -sine_table
    ).reshape(row_count, D)
    grad_key_rows = rotate(
        grad_tokens[1].astype(jnp.float32).reshape(row_count, HEADS, HEAD), cosine, -sine_table
    ).reshape(row_count, D)
    grad_proj = jnp.concatenate(
        [grad_query_rows, grad_key_rows, grad_tokens[2].astype(jnp.float32)], axis=1
    ).astype(jnp.bfloat16)
    grad_attn_in = contract_cols(
        grad_proj, lax.all_gather(qkv_weight, ("dp", "sp"), axis=0, tiled=True)
    )
    hidden_cols = gelu_value(stored).astype(jnp.bfloat16)
    grad_up = contract_rows(grad_pre, mlp_in).reshape(
        lax.axis_size(("dp", "sp")) * local_rows, 4 * D
    )
    grad_down = contract_rows(hidden_cols, grad_out).reshape(
        lax.axis_size(("dp", "sp")) * local_rows, 4 * D
    )
    grad_qkv = contract_rows(attn_in, grad_proj)
    grad_dense = contract_rows(context, grad_out)
    every_grad = lax.psum_scatter(
        jnp.concatenate(
            [
                jnp.concatenate([grad_qkv, grad_dense], axis=1),
                jnp.concatenate([grad_up, grad_down], axis=1),
            ],
            axis=1,
        ),
        ("dp", "sp"),
        scatter_dimension=0,
        tiled=True,
    )
    qkv_grad = every_grad[:, : 3 * D]
    dense_grad = every_grad[:, 3 * D : 4 * D]
    up_grad = every_grad[:, 4 * D : 8 * D].reshape(4 * local_rows, D)
    down_grad = every_grad[:, 8 * D :].reshape(4 * local_rows, D)
    qkv_bias_part = jnp.sum(grad_proj, axis=0, dtype=jnp.float32).reshape(3, D)
    unit_grad = jnp.sum(grad_pre, axis=0, dtype=jnp.float32)
    out_bias_grad = jnp.sum(grad_out, axis=0, dtype=jnp.float32)
    gain_grad = jnp.stack(
        [jnp.sum(grad_attn_in * normed, axis=0), jnp.sum(grad_mlp_in * normed, axis=0)]
    )
    shift_grad = jnp.stack([jnp.sum(grad_attn_in, axis=0), jnp.sum(grad_mlp_in, axis=0)])
    gain_total, shift_total, qkv_bias_total, unit_total, out_bias_total = lax.psum(
        (gain_grad, shift_grad, qkv_bias_part, unit_grad, out_bias_grad), ("dp", "sp")
    )
    grad_hat = grad_attn_in * gains[0] + grad_mlp_in * gains[1]
    grad_input = inverse * (
        grad_hat
        - jnp.mean(grad_hat, axis=-1, keepdims=True)
        - normed * jnp.mean(grad_hat * normed, axis=-1, keepdims=True)
    )
    input_grad = (grad_out.astype(jnp.float32) + grad_input).astype(jnp.bfloat16)
    return (
        output,
        input_grad,
        gain_total,
        shift_total,
        qkv_grad,
        qkv_bias_total,
        dense_grad,
        up_grad,
        unit_total,
        down_grad,
        out_bias_total,
    )


def solution(mesh):
    return jax.shard_map(
        body,
        mesh=mesh,
        in_specs=(
            P(("dp", "sp"), None),
            P("dp"),
            P(("dp", "sp"), None),
            P(),
            P(),
            P(("dp", "sp"), None),
            P(),
            P(("dp", "sp"), None),
            P(("dp", "sp"), None),
            P(),
            P(("dp", "sp"), None),
            P(),
        ),
        out_specs=(
            P(("dp", "sp"), None),
            P(("dp", "sp"), None),
            P(),
            P(),
            P(("dp", "sp"), None),
            P(),
            P(("dp", "sp"), None),
            P(("dp", "sp"), None),
            P(),
            P(("dp", "sp"), None),
            P(),
        ),
        check_vma=False,
    )
```

profile of v0, /device:TPU:8, one launch (start us, length us, event | category | flops | bytes accessed | tf_op | source)
XLA Modules:
  0.0 2947.8 jit_solution(1488606801998908065)
XLA Ops:
  8.7 2.8 reshape.341
  16.1 148.8 %all-gather.5.cloned.1.call-done = bf16[2048,6144]{1,0:T(8,128)(2,1)} async-done(((bf16[64,6144]{1,0:T(8,128)(2,1)}), bf16[2048,6144]{1,0:T(8,128)(2,1)}) %all-gather.5.cloned.1.call-update) | async-done | bytes 25165840 | tf_op jit(solution)/shard_map/all_gather | solution.py:191
  164.9 11.8 convolution_add_fusion.1
  177.1 2.5 copy-done.18
  184.9 2.3 copy.175
  193.2 1.8 subtract_convert_fusion.3
  197.2 2.2 pad_maximum_fusion.4
  205.6 1.9 pad_maximum_fusion.1
  207.5 4.8 copy.138
  212.3 7.5 all-to-all-start
  220.5 50.5 %all-gather.7.cloned.1.call-done = bf16[2048,2048]{1,0:T(8,128)(2,1)} async-done(((bf16[64,2048]{1,0:T(8,128)(2,1)}), bf16[2048,2048]{1,0:T(8,128)(2,1)}) %all-gather.7.cloned.1.call-update) | async-done | bytes 8388624 | tf_op jit(solution)/shard_map/all_gather | solution.py:218
  271.0 5.8 convolution_convert_fusion
  277.8 81.2 %all-to-all-done = bf16[3,256,2048]{1,0,2:T(4,128)(2,1)} async-done(((bf16[3,256,2048]{1,0,2:T(4,128)(2,1)}), bf16[3,256,2048]{1,0,2:T(4,128)(2,1)}, u32[]{:S(2)}, u32[]{:S(2)}) %all-to-all-start) | async-done | bytes 3145760 | tf_op jit(solution)/shard_map/all_to_all | solution.py:211
  359.0 8.3 all-to-all-start.2
  367.4 7.1 copy.139
  374.5 3.6 fusion.62
  379.4 2.5 reshape.355
  382.0 2.3 copy.163
  384.2 2.3 copy.142
  386.6 2.5 copy.143
  389.0 24.9 while.27
  394.7 2.7 fusion.116
  398.6 1.8 fusion.118
  407.1 2.7 fusion.116
  413.9 3.7 copy.164
  417.6 2.3 copy.148
  419.9 5.3 all-to-all-start.1
  425.2 42.3 %while.28 = (s32[]{:T(128)}, f32[1024,2,256]{0,2,1:T(8,128)S(1)}, f32[1024,2,256]{0,2,1:T(8,128)}, bf16[2,512,512]{2,1,0:T(8,128)(2,1)}, s32[2]{0:T(128)S(1)}, /...) while((s32[]{:T(128)}, f32[1024,2,256]{0,2,1:T(8,128)S(1)}, ...), condition=%wide.region_8.9_spmd.clone, body=%wide.region_6.8_spmd.clone.sunk | while | flops 2704278016 | bytes 61376784 | solution.py:149
  429.6 2.1 constant_dynamic-slice_fusion.8
  434.3 2.0 fusion.129
  436.3 2.8 bitcast_add_fusion.5
  439.2 2.2 multiply_reduce_fusion.2
  449.9 2.0 constant_dynamic-slice_fusion.8
  454.5 2.0 fusion.129
  456.5 4.6 bitcast_add_fusion.5
  461.0 2.2 multiply_reduce_fusion.2
  472.1 4.7 copy.152
  477.3 8.3 all-to-all-start.3
  485.6 1.9 copy.145
  487.5 8.2 fusion.55
  495.7 131.5 %all-to-all-done.3 = bf16[3,1024,512]{2,0,1:T(4,128)(2,1)} async-done(((bf16[3,1024,512]{2,0,1:T(4,128)(2,1)}), bf16[3,1024,512]{2,0,1:T(4,128)(2,1)}, u32[]{:S(2)}, u32[]{:S(2)}) %all-to-all-start.3) | async-done | bytes 3145760 | tf_op jit(solution)/shard_map/all_to_all | solution.py:243
  627.2 3.1 copy.153
  645.1 20.5 fusion.50
  665.6 55.4 %reshape.342 = bf16[8192,2048]{1,0:T(8,128)(2,1)} reshape(bf16[2048,8192]{1,0:T(8,128)(2,1)} %all-gather.9.cloned.1.call-done) | data formatting | bytes 67108864 | tf_op jit(solution)/shard_map/reshape | solution.py:196
  721.0 19.3 convolution_add_fusion
  740.3 27.6 fusion.54
  767.9 46.2 %all-gather.11.cloned.1.call-done = bf16[2048,8192]{1,0:T(8,128)(2,1)} async-done(((bf16[64,8192]{1,0:T(8,128)(2,1)}), bf16[2048,8192]{1,0:T(8,128)(2,1)}) %all-gather.11.cloned.1.call-update) | async-done | bytes 33554448 | tf_op jit(solution)/shard_map/all_gather | solution.py:193
  814.1 55.1 %reshape.344 = bf16[8192,2048]{1,0:T(8,128)(2,1)} reshape(bf16[2048,8192]{1,0:T(8,128)(2,1)} %all-gather.11.cloned.1.call-done) | data formatting | bytes 67108864 | tf_op jit(solution)/shard_map/reshape | solution.py:197
  869.2 20.3 convert_reduce_fusion
  889.6 79.3 %reshape.348 = f32[2048,8192]{1,0:T(8,128)} reshape(f32[8192,2048]{1,0:T(8,128)} %fusion.54) | data formatting | bytes 134217728 | tf_op jit(solution)/shard_map/reshape | solution.py:260
  968.9 25.5 fusion.47
  994.4 79.3 %reshape.347 = f32[2048,8192]{1,0:T(8,128)} reshape(f32[8192,2048]{1,0:T(8,128)} %fusion.47) | data formatting | bytes 134217728 | tf_op jit(solution)/shard_map/reshape | solution.py:257
  1073.7 130.5 %pad_maximum_fusion = f32[2048,24576]{1,0:T(8,128)} fusion(f32[2048,8192]{1,0:T(8,128)} %reshape.348, f32[2048,8192]{1,0:T(8,128)} %reshape.347, f32[2048,2048]{1,0:T(8,128)} %fusion.55, f32[2048,6144]{1,0:T(8,128)} %fusion.50), kind=kLoop, calls=%fused_computation.38 | loop fusion | flops 150994944 | bytes 402653184 | tf_op jit(solution)/shard_map/concatenate | solution.py:266
  1205.8 7.2 convert_add_fusion
  1214.7 25.1 fusion.68
  1239.8 20.2 fusion.56
  1261.2 4.6 convert_reduce_fusion.3
  1265.8 31.0 %fusion.24 = bf16[256,2048]{1,0:T(8,128)(2,1)} fusion(f32[256,2048]{1,0:T(8,128)S(1)} %copy-done.20, bf16[8192,2048]{1,0:T(8,128)(2,1)} %reshape.344, f32[2048]{0:T(1024)S(1)} %convert_element_type.122, f32[256,8192]{1,0:T(8,128)} %convolution_add_fusion), kind=kOutput, calls=%fused_computation.61 | convolution fusion | flops 8601993216 | bytes 45096960 | tf_op jit(solution)/shard_map/dot_general | solution.py:200
  1296.9 1504.9 %reduce-scatter.2.cloned.1.call-done = f32[64,24576]{1,0:T(8,128)} async-done(((f32[2048,24576]{1,0:T(8,128)}), f32[64,24576]{1,0:T(8,128)}) %reduce-scatter.2.cloned.1.call-update) | async-done | bytes 6291472 | tf_op jit(solution)/shard_map/reduce_scatter | solution.py:265
  2801.8 3.9 fusion.59
  2805.7 2.9 reshape.351
  2810.2 1.9 slice.158
  2812.0 2.7 slice.157
  2814.7 119.1 %all-reduce.3.cloned.1.call-done = (f32[2,2048]{1,0:T(2,128)}, f32[2,2048]{1,0:T(2,128)}, f32[3,2048]{1,0:T(4,128)}, f32[8192]{0:T(1024)}, f32[2048]{0:T(1024)}) async-done(((f32[2,2048]{1,0:T(2,128)}, f32[2,2048]{1,0:T(2,128)}, f32[3,2048]{1,0:T(4,128)}, f32[8192]{0:T(1024)}, f32[2048]{0:T(1024)}), (f32[2,2048]{1,0:T(2,128)}, f32[2,2048]{1,0:T(2,128)}, f32[3,2048]{1,0:T(4,128)}, f32[8192]{0:T(1024)}, ...) | async-done | bytes 98320 | tf_op jit(solution)/shard_map/psum | solution.py:288
  (224 shorter events, 92.9 us)
Async XLA Ops:
  7.2 4.4 copy-start.21
  7.2 157.7 %all-gather.5.cloned.1.call-start = ((), (), s32[]{:S(2)}) async-start(), calls=%async_computation.5 | async-start | bytes 25952256 | tf_op jit(solution)/shard_map/all_gather | solution.py:191
  7.9 263.0 %all-gather.7.cloned.1.call-start = ((), (), s32[]{:S(2)}) async-start(), calls=%async_computation.6 | async-start | bytes 8650752 | tf_op jit(solution)/shard_map/all_gather | solution.py:218
  8.7 4.6 copy-start.45
  8.7 4.6 copy-start
  8.7 656.9 %all-gather.9.cloned.1.call-start = ((), (), s32[]{:S(2)}) async-start(), calls=%async_computation.7 | async-start | bytes 34603008 | tf_op jit(solution)/shard_map/all_gather | solution.py:192
  11.5 3.3 copy-start.40
  11.5 4.0 copy-start.41
  11.5 802.5 %all-gather.11.cloned.1.call-start = ((), (), s32[]{:S(2)}) async-start(), calls=%async_computation.8 | async-start | bytes 34603008 | tf_op jit(solution)/shard_map/all_gather | solution.py:193
  13.6 163.2 %copy-start.30 = (f32[256]{0:T(256)}, f32[256]{0:T(256)S(1)}, u32[]{:S(2)}) copy-start(f32[256]{0:T(256)S(1)} %broadcast_multiply_fusion.2) | copy-start | bytes 3076
  14.0 162.8 %copy-start.34 = (f32[256]{0:T(256)}, f32[256]{0:T(256)S(1)}, u32[]{:S(2)}) copy-start(f32[256]{0:T(256)S(1)} %add_rsqrt_fusion) | copy-start | bytes 3076
  15.5 161.3 %copy-start.23 = (f32[1,2048]{1,0:T(1,128)}, f32[1,2048]{1,0:T(1,128)S(1)}, u32[]{:S(2)}) copy-start(f32[1,2048]{1,0:T(1,128)S(1)} %get-tuple-element.345) | copy-start | bytes 24580
  16.1 160.7 %copy-start.26 = (f32[1,2048]{1,0:T(1,128)}, f32[1,2048]{1,0:T(1,128)S(1)}, u32[]{:S(2)}) copy-start(f32[1,2048]{1,0:T(1,128)S(1)} %get-tuple-element.347) | copy-start | bytes 24580
  176.8 2.8 copy-start.18
  190.1 7.1 copy-start.19
  195.0 5.8 copy-start.28
  212.3 58.7 %copy-start.7 = (bf16[256,2048]{1,0:T(8,128)(2,1)S(1)}, bf16[256,2048]{1,0:T(8,128)(2,1)}, u32[]{:S(2)}) copy-start(bf16[256,2048]{1,0:T(8,128)(2,1)} %param.18) | copy-start | bytes 3145732
  212.3 146.8 %all-to-all-start = ((bf16[3,256,2048]{1,0,2:T(4,128)(2,1)}), bf16[3,256,2048]{1,0,2:T(4,128)(2,1)}, u32[]{:S(2)}, u32[]{:S(2)}) async-start(bf16[3,256,2048]{1,0,2:T(4,128)(2,1)} %copy.138), calls=%async_computation | async-start | bytes 8388608 | tf_op jit(solution)/shard_map/all_to_all | solution.py:211
  220.5 648.7 %copy-start.42 = (f32[256]{0:T(256)}, f32[256]{0:T(256)S(1)}, u32[]{:S(2)}) copy-start(f32[256]{0:T(256)S(1)} %compare_convert_fusion) | copy-start | bytes 3076
  359.0 60.9 %all-to-all-start.2 = ((bf16[256,4,512]{2,0,1:T(8,128)(2,1)}), bf16[256,4,512]{2,0,1:T(8,128)(2,1)}, u32[]{:S(2)}, u32[]{:S(2)}) async-start(bf16[256,4,512]{2,0,1:T(8,128)(2,1)} %bitcast.85), calls=%async_computation.2 | async-start | bytes 2097152 | tf_op jit(solution)/shard_map/all_to_all | solution.py:236
  379.4 7.2 copy-start.17
  397.4 1.2 copy-start.22
  409.8 1.2 copy-start.22
  419.9 57.4 %all-to-all-start.1 = ((bf16[4,256,512]{2,1,0:T(8,128)(2,1)}), bf16[4,256,512]{2,1,0:T(8,128)(2,1)}, u32[]{:S(2)}, u32[]{:S(2)}) async-start(bf16[4,256,512]{2,1,0:T(8,128)(2,1)} %bitcast.12), calls=%async_computation.1 | async-start | bytes 2097152 | tf_op jit(solution)/shard_map/all_to_all | solution.py:215
  436.3 2.8 copy-start.3
  441.3 1.3 copy-start.4
  456.4 4.6 copy-start.3
  463.2 1.3 copy-start.4
  476.8 8.8 copy-start.44
  476.8 10.7 copy-start.8
  477.3 149.9 %all-to-all-start.3 = ((bf16[3,1024,512]{2,0,1:T(4,128)(2,1)}), bf16[3,1024,512]{2,0,1:T(4,128)(2,1)}, u32[]{:S(2)}, u32[]{:S(2)}) async-start(bf16[3,1024,512]{2,0,1:T(4,128)(2,1)} %copy.152), calls=%async_computation.3 | async-start | bytes 8388608 | tf_op jit(solution)/shard_map/all_to_all | solution.py:243
  485.6 2316.2 %reduce-scatter.2.cloned.1.call-start = ((), (), s32[]{:S(2)}) async-start(), calls=%async_computation.9 | async-start | bytes 207618048 | tf_op jit(solution)/shard_map/reduce_scatter | solution.py:265
  487.5 8.3 copy-start.5
  636.4 4.0 copy-start.29
  636.4 4.0 copy-start.33
  640.4 25.2 copy-start.10
  640.4 4.7 copy-start.1
  640.4 4.7 copy-start.24
  640.4 4.7 copy-start.27
  640.4 4.7 copy-start.31
  640.4 4.7 copy-start.35
  643.8 1.0 copy-start.12
  643.8 1.3 copy-start.15
  665.6 55.4 %copy-start.37 = (f32[1,2048]{1,0:T(1,128)S(1)}, f32[1,2048]{1,0:T(1,128)}, u32[]{:S(2)}) copy-start(f32[1,2048]{1,0:T(1,128)} %get-tuple-element.344) | copy-start | bytes 24580
  665.6 55.4 %copy-start.39 = (f32[1,2048]{1,0:T(1,128)S(1)}, f32[1,2048]{1,0:T(1,128)}, u32[]{:S(2)}) copy-start(f32[1,2048]{1,0:T(1,128)} %get-tuple-element.346) | copy-start | bytes 24580
  1204.2 0.7 copy-start.46
  1204.2 1.2 copy-start.2
  1204.2 1.5 copy-start.6
  1204.3 1729.6 %all-reduce.3.cloned.1.call-start = ((), (), s32[]{:S(2)}) async-start(), calls=%async_computation.10 | async-start | bytes 212992 | tf_op jit(solution)/shard_map/psum | solution.py:288
  1205.8 7.2 copy-start.11
  1205.8 7.2 copy-start.13
  1205.8 7.2 copy-start.16
  1214.6 25.1 copy-start.14
  1214.6 25.1 copy-start.25
  1214.6 25.1 copy-start.32
  1214.6 25.1 copy-start.36
  1214.6 25.1 copy-start.38
  1239.8 21.5 copy-start.9
  1239.8 21.5 copy-start.43
  1259.9 5.9 copy-start.20
Sparse Core Ops, SparseCore 0:
  10.9 153.9 all-gather.4
  167.8 103.0 all-gather.6
  273.9 339.1 all-gather.8
  615.8 198.1 all-gather.10
  1204.4 1597.3 reduce-scatter.1
  2809.2 124.5 all-reduce.2
where the time goes:
time: 2960 us; the launch traced here: 2950 us
  waiting for transfers between devices  2080 us (70%)
  local copies, waits for them, and re-layouts  391 us (13%)
  matrix products  251 us (8%)
  other arithmetic  167 us (6%)
  starting transfers between devices  29.8 us (1%)
    reduce_scatter x1, waiting for transfers between devices, body(): lax.psum_scatter(jnp.concatenate([jnp.concatenate([grad_qkv, grad_dense],...  1500 us
    all_gather x1, waiting for transfers between devices, body(): qkv_piece = lax.all_gather(qkv_weight, ('dp', 'sp'), axis=0, tiled=True)  149 us
    all_to_all x1, waiting for transfers between devices, body(): lax.all_to_all(grad_packed, 'sp', split_axis=1, concat_axis=2, tiled=True)  132 us
    concatenate x1, other arithmetic, body(): jnp.concatenate([jnp.concatenate([grad_qkv, grad_dense], axis=1), jnp.con...  130 us
    psum x1, waiting for transfers between devices, body(): lax.psum((gain_grad, shift_grad, qkv_bias_part, unit_grad, out_bias_grad)...  119 us
    dot_general x4, matrix products, contract_rows(): lax.dot_general(left, right, (((0,), (0,)), ((), ())), preferred_element_...  81.8 us
    all_to_all x1, waiting for transfers between devices, body(): lax.all_to_all(packed, 'sp', split_axis=2, concat_axis=1, tiled=True)  81.2 us
    reshape x1, local copies, waits for them, and re-layouts, body(): contract_rows(grad_pre, mlp_in)  79.3 us
  transfers between devices with their start and end apart: 10, of which 8 were waited for; matrix products, arithmetic and copies ran while one was open for 14% of the time, Pallas kernels for 0%

commit v1 on v0

--- a/solution.py
+++ b/solution.py
@@ -170,142 +170,189 @@
     down_weight,
     out_bias,
 ):
-    row_count = tokens.shape[0]
-    local_rows = qkv_weight.shape[0]
+    dp_size = lax.axis_size("dp")
+    sp_size = lax.axis_size("sp")
+    shard = lax.axis_index("sp")
+    own_rows = tokens.shape[0]
+    seq_rows = own_rows * sp_size
+    head_width = D // sp_size
     score_scale = HEAD ** (-0.5)
     length = lengths[0]
-    positions = lax.axis_index("sp") * row_count + jnp.arange(row_count, dtype=jnp.int32)
+    low = jnp.bfloat16
+    full = jnp.float32
+
+    seq_tokens = lax.all_gather(tokens, "sp", axis=0, tiled=True)
+    seq_cotangent = lax.all_gather(cotangent, "sp", axis=0, tiled=True)
+    qkv_rows = qkv_weight.shape[0]
+    qkv_slab = lax.all_to_all(
+        qkv_weight.reshape(qkv_rows, 3, sp_size, head_width),
+        "sp",
+        split_axis=2,
+        concat_axis=0,
+        tiled=True,
+    )
+    qkv_own = lax.all_gather(
+        qkv_slab.reshape(qkv_rows * sp_size, 3 * head_width), "dp", axis=0, tiled=True
+    )
+    up_own = lax.all_gather(up_weight, "dp", axis=0, tiled=True)
+    down_own = lax.all_gather(down_weight, "dp", axis=0, tiled=True)
+    out_blocks = lax.all_gather(out_weight, "dp", axis=0, tiled=True)
+    per_shard = dp_size // sp_size
+    out_own = lax.all_to_all(
+        out_blocks.reshape(sp_size, per_shard, qkv_rows, D),
+        "sp",
+        split_axis=0,
+        concat_axis=2,
+        tiled=True,
+    ).reshape(head_width, D)
+    units = up_weight.shape[0]
+    unit_bias = lax.dynamic_index_in_dim(
+        up_bias.reshape(dp_size, sp_size, units), shard, 1, keepdims=False
+    ).reshape(dp_size * units)
+    bias_own = lax.dynamic_index_in_dim(
+        qkv_bias.reshape(3, sp_size, head_width), shard, 1, keepdims=False
+    ).reshape(3 * head_width)
+
+    positions = jnp.arange(seq_rows, dtype=jnp.int32)
     cosine, sine_table = rotary_tables(positions)
-    inputs = tokens.astype(jnp.float32)
-    gains = ln_gains.astype(jnp.float32)
-    shifts = ln_shifts.astype(jnp.float32)
+    gains = ln_gains.astype(full)
+    shifts = ln_shifts.astype(full)
+    inputs = seq_tokens.astype(full)
     centre = jnp.mean(inputs, axis=-1, keepdims=True)
     centered = inputs - centre
     inverse = lax.rsqrt(jnp.mean(centered * centered, axis=-1, keepdims=True) + eps)
     normed = centered * inverse
-    attn_in = (normed * gains[0] + shifts[0]).astype(jnp.bfloat16)
-    mlp_in = (normed * gains[1] + shifts[1]).astype(jnp.bfloat16)
-    unit_bias = up_bias.astype(jnp.float32)
-    up_flat = up_weight.reshape(local_rows, 4 * D)
-    down_flat = down_weight.reshape(local_rows, 4 * D)
-    qkv_piece = lax.all_gather(qkv_weight, ("dp", "sp"), axis=0, tiled=True)
-    up_piece = lax.all_gather(up_flat, ("dp", "sp"), axis=0, tiled=True)
-    down_piece = lax.all_gather(down_flat, ("dp", "sp"), axis=0, tiled=True)
-    piece_rows = qkv_piece.shape[0]
-    projected = jnp.dot(attn_in, qkv_piece, preferred_element_type=jnp.float32)
-    up_rows = up_piece.reshape(4 * piece_rows, D)
-    down_rows = down_piece.reshape(4 * piece_rows, D)
-    pre_act = contract_cols(mlp_in, up_rows) + unit_bias
-    hidden = gelu_value(pre_act).astype(jnp.bfloat16)
-    mlp_out = jnp.dot(hidden, down_rows, preferred_element_type=jnp.float32)
-    front_stored = pre_act
-    projected, stored, mlp_out = (projected, front_stored, mlp_out)
-    projected = projected + qkv_bias.astype(jnp.float32).reshape(3 * D)
-    queries = rotate(projected[:, :D].reshape(row_count, HEADS, HEAD), cosine, sine_table).reshape(
-        row_count, D
-    )
-    key_rows = rotate(
-        projected[:, D : 2 * D].reshape(row_count, HEADS, HEAD), cosine, sine_table
-    ).reshape(row_count, D)
-    packed = jnp.stack([queries, key_rows, projected[:, 2 * D :]]).astype(jnp.bfloat16)
-    head_major = lax.all_to_all(packed, "sp", split_axis=2, concat_axis=1, tiled=True)
-    context_heads, log_sums = attend_forward(
-        head_major[0], head_major[1], head_major[2], length, score_scale
-    )
-    context = lax.all_to_all(context_heads, "sp", split_axis=0, concat_axis=1, tiled=True)
-    attn_out = jnp.dot(
-        context,
-        lax.all_gather(out_weight, ("dp", "sp"), axis=0, tiled=True),
-        preferred_element_type=jnp.float32,
-    )
-    output = (inputs + attn_out + mlp_out + out_bias.astype(jnp.float32)).astype(jnp.bfloat16)
-    row_valid = (positions < length).astype(jnp.float32)
-    grad_out = (cotangent.astype(jnp.float32) * row_valid[:, None]).astype(jnp.bfloat16)
-    out_piece = lax.all_gather(out_weight, ("dp", "sp"), axis=0, tiled=True)
-    up_piece = lax.all_gather(up_flat, ("dp", "sp"), axis=0, tiled=True)
-    down_piece = lax.all_gather(down_flat, ("dp", "sp"), axis=0, tiled=True)
-    piece_rows = out_piece.shape[0]
-    grad_context = contract_cols(grad_out, out_piece)
-    up_rows = up_piece.reshape(4 * piece_rows, D)
-    down_rows = down_piece.reshape(4 * piece_rows, D)
-    grad_hidden = contract_cols(grad_out, down_rows)
-    pre_act = stored
-    grad_low = (grad_hidden * gelu_slope(pre_act)).astype(jnp.bfloat16)
-    grad_mlp_in = jnp.dot(grad_low, up_rows, preferred_element_type=jnp.float32)
-    grad_context, grad_mlp_in, grad_pre = (grad_context, grad_mlp_in, grad_low)
-    grad_heads = lax.all_to_all(
-        grad_context.astype(jnp.bfloat16), "sp", split_axis=1, concat_axis=0, tiled=True
-    )
+    attn_in = (normed * gains[0] + shifts[0]).astype(low)
+    mlp_in = (normed * gains[1] + shifts[1]).astype(low)
+    row_valid = positions < length
+    grad_out = jnp.where(row_valid[:, None], seq_cotangent, jnp.zeros_like(seq_cotangent))
+
+    heads_own = head_width // HEAD
+    projected = jnp.dot(attn_in, qkv_own, preferred_element_type=full) + bias_own.astype(full)
+    queries = (
+        rotate(projected[:, :head_width].reshape(seq_rows, heads_own, HEAD), cosine, sine_table)
+        .reshape(seq_rows, head_width)
+        .astype(low)
+    )
+    key_rows = (
+        rotate(
+            projected[:, head_width : 2 * head_width].reshape(seq_rows, heads_own, HEAD),
+            cosine,
+            sine_table,
+        )
+        .reshape(seq_rows, head_width)
+        .astype(low)
+    )
+    values = projected[:, 2 * head_width :].astype(low)
+    context, log_sums = attend_forward(queries, key_rows, values, length, score_scale)
+
+    pre_act = contract_cols(mlp_in, up_own) + unit_bias.astype(full)
+    hidden = gelu_value(pre_act).astype(low)
+    partial_out = jnp.dot(hidden, down_own, preferred_element_type=full) + jnp.dot(
+        context, out_own, preferred_element_type=full
+    )
+    reduced_out = lax.psum_scatter(
+        partial_out.astype(low), "sp", scatter_dimension=0, tiled=True
+    )
+    output = (
+        tokens.astype(full) + reduced_out.astype(full) + out_bias.astype(full)
+    ).astype(low)
+
+    grad_hidden = contract_cols(grad_out, down_own)
+    grad_pre = (grad_hidden * gelu_slope(pre_act)).astype(low)
+    grad_down = lax.psum_scatter(
+        contract_rows(hidden, grad_out).astype(low), "dp", scatter_dimension=0, tiled=True
+    )
+    grad_up = lax.psum_scatter(
+        contract_rows(grad_pre, mlp_in).astype(low), "dp", scatter_dimension=0, tiled=True
+    )
+    grad_mlp_in = jnp.dot(grad_pre, up_own, preferred_element_type=full)
+
+    grad_context = contract_cols(grad_out, out_own).astype(low)
+    grad_dense = contract_rows(context, grad_out).astype(low)
+    grad_dense = lax.all_to_all(
+        grad_dense.reshape(per_shard, sp_size, qkv_rows, D),
+        "sp",
+        split_axis=1,
+        concat_axis=0,
+        tiled=True,
+    ).reshape(dp_size * qkv_rows, D)
+    grad_dense = lax.psum_scatter(grad_dense, "dp", scatter_dimension=0, tiled=True)
     grad_queries, grad_keys, grad_values = attend_backward(
-        head_major[0], head_major[1], head_major[2], grad_heads, log_sums, length, score_scale
-    )
-    grad_packed = jnp.stack([grad_queries, grad_keys, grad_values]).astype(jnp.bfloat16)
-    grad_tokens = lax.all_to_all(grad_packed, "sp", split_axis=1, concat_axis=2, tiled=True)
-    grad_query_rows = rotate(
-        grad_tokens[0].astype(jnp.float32).reshape(row_count, HEADS, HEAD), cosine, -sine_table
-    ).reshape(row_count, D)
-    grad_key_rows = rotate(
-        grad_tokens[1].astype(jnp.float32).reshape(row_count, HEADS, HEAD), cosine, -sine_table
-    ).reshape(row_count, D)
+        queries, key_rows, values, grad_context, log_sums, length, score_scale
+    )
+
+    def turn_back(grad):
+        return (
+            rotate(
+                grad.astype(low).astype(full).reshape(seq_rows, heads_own, HEAD),
+                cosine,
+                -sine_table,
+            )
+            .reshape(seq_rows, head_width)
+            .astype(low)
+        )
+
     grad_proj = jnp.concatenate(
-        [grad_query_rows, grad_key_rows, grad_tokens[2].astype(jnp.float32)], axis=1
-    ).astype(jnp.bfloat16)
-    grad_attn_in = contract_cols(
-        grad_proj, lax.all_gather(qkv_weight, ("dp", "sp"), axis=0, tiled=True)
-    )
-    hidden_cols = gelu_value(stored).astype(jnp.bfloat16)
-    grad_up = contract_rows(grad_pre, mlp_in).reshape(
-        lax.axis_size(("dp", "sp")) * local_rows, 4 * D
-    )
-    grad_down = contract_rows(hidden_cols, grad_out).reshape(
-        lax.axis_size(("dp", "sp")) * local_rows, 4 * D
-    )
-    grad_qkv = contract_rows(attn_in, grad_proj)
-    grad_dense = contract_rows(context, grad_out)
-    every_grad = lax.psum_scatter(
-        jnp.concatenate(
-            [
-                jnp.concatenate([grad_qkv, grad_dense], axis=1),
-                jnp.concatenate([grad_up, grad_down], axis=1),
-            ],
-            axis=1,
-        ),
-        ("dp", "sp"),
-        scatter_dimension=0,
+        [turn_back(grad_queries), turn_back(grad_keys), grad_values.astype(low)], axis=1
+    )
+    grad_attn_in = contract_cols(grad_proj, qkv_own)
+    grad_hat = grad_attn_in * gains[0] + grad_mlp_in * gains[1]
+    reduced_hat = lax.psum_scatter(
+        grad_hat.astype(low), "sp", scatter_dimension=0, tiled=True
+    ).astype(full)
+    grad_qkv = lax.psum_scatter(
+        contract_rows(attn_in, grad_proj).astype(low), "dp", scatter_dimension=0, tiled=True
+    )
+    grad_qkv = lax.all_to_all(
+        grad_qkv.reshape(sp_size, qkv_rows, 3, 1, head_width),
+        "sp",
+        split_axis=0,
+        concat_axis=3,
         tiled=True,
-    )
-    qkv_grad = every_grad[:, : 3 * D]
-    dense_grad = every_grad[:, 3 * D : 4 * D]
-    up_grad = every_grad[:, 4 * D : 8 * D].reshape(4 * local_rows, D)
-    down_grad = every_grad[:, 8 * D :].reshape(4 * local_rows, D)
-    qkv_bias_part = jnp.sum(grad_proj, axis=0, dtype=jnp.float32).reshape(3, D)
-    unit_grad = jnp.sum(grad_pre, axis=0, dtype=jnp.float32)
-    out_bias_grad = jnp.sum(grad_out, axis=0, dtype=jnp.float32)
+    ).reshape(qkv_rows, 3 * D)
+
+    own_cotangent = lax.dynamic_slice_in_dim(grad_out, shard * own_rows, own_rows, 0).astype(full)
+    spread_units = lax.dynamic_update_index_in_dim(
+        jnp.zeros((dp_size, sp_size, units), full),
+        jnp.sum(grad_pre, axis=0, dtype=full).reshape(dp_size, units),
+        shard,
+        1,
+    ).reshape(-1)
+    spread_bias = lax.dynamic_update_index_in_dim(
+        jnp.zeros((3, sp_size, head_width), full),
+        jnp.sum(grad_proj, axis=0, dtype=full).reshape(3, head_width),
+        shard,
+        1,
+    ).reshape(3, D)
     gain_grad = jnp.stack(
         [jnp.sum(grad_attn_in * normed, axis=0), jnp.sum(grad_mlp_in * normed, axis=0)]
     )
     shift_grad = jnp.stack([jnp.sum(grad_attn_in, axis=0), jnp.sum(grad_mlp_in, axis=0)])
     gain_total, shift_total, qkv_bias_total, unit_total, out_bias_total = lax.psum(
-        (gain_grad, shift_grad, qkv_bias_part, unit_grad, out_bias_grad), ("dp", "sp")
-    )
-    grad_hat = grad_attn_in * gains[0] + grad_mlp_in * gains[1]
-    grad_input = inverse * (
-        grad_hat
-        - jnp.mean(grad_hat, axis=-1, keepdims=True)
-        - normed * jnp.mean(grad_hat * normed, axis=-1, keepdims=True)
-    )
-    input_grad = (grad_out.astype(jnp.float32) + grad_input).astype(jnp.bfloat16)
+        (gain_grad, shift_grad, spread_bias, spread_units, jnp.sum(own_cotangent, axis=0)),
+        ("dp", "sp"),
+    )
+
+    own_inverse = lax.dynamic_slice_in_dim(inverse, shard * own_rows, own_rows, 0)
+    own_normed = lax.dynamic_slice_in_dim(normed, shard * own_rows, own_rows, 0)
+    grad_input = own_inverse * (
+        reduced_hat
+        - jnp.mean(reduced_hat, axis=-1, keepdims=True)
+        - own_normed * jnp.mean(reduced_hat * own_normed, axis=-1, keepdims=True)
+    )
+    input_grad = (own_cotangent + grad_input).astype(low)
     return (
         output,
         input_grad,
         gain_total,
         shift_total,
-        qkv_grad,
+        grad_qkv.astype(full),
         qkv_bias_total,
-        dense_grad,
-        up_grad,
+        grad_dense.astype(full),
+        grad_up.astype(full),
         unit_total,
-        down_grad,
+        grad_down.astype(full),
         out_bias_total,
     )
 

time: 2960 us -> 1030 us (0.35)
  waiting for transfers between devices: 2080 us -> 624 us
  local copies, waits for them, and re-layouts: 391 us -> 77.7 us
  other arithmetic: 167 us -> 72.8 us
  matrix products: 251 us -> 189 us
    reduce_scatter x1 -> x6, waiting for transfers between devices: 1500 us -> 227 us  [the longest x1 72.7 us: body(): lax.psum_scatter(contract_rows(grad_pre, mlp_in).astype(low), 'dp', scatt...]
    reshape x9 -> x10, local copies, waits for them, and re-layouts: 279 us -> 17.8 us  [the longest x2 5.87 us: body(): grad_qkv.reshape(sp_size, qkv_rows, 3, 1, head_width)]
    all_to_all x4 -> x3, waiting for transfers between devices: 213 us -> 41.7 us  [the longest x1 32.2 us: body(): lax.all_to_all(grad_qkv.reshape(sp_size, qkv_rows, 3, 1, head_width), 'sp...]
    concatenate x1 -> x0, other arithmetic: 130 us -> none  [body(): jnp.concatenate([jnp.concatenate([grad_qkv, grad_dense], axis=1), jnp.con...]
    dot_general x4, matrix products: 81.8 us -> 47.3 us  [contract_rows(): lax.dot_general(left, right, (((0,), (0,)), ((), ())), preferred_element_...]
    dot_general x4, matrix products: 75.2 us -> 43 us  [the longest x1 15 us: body(): grad_mlp_in = jnp.dot(grad_pre, up_own, preferred_element_type=full)]
    all_gather x4 -> x6, waiting for transfers between devices: 246 us -> 222 us  [the longest x1 108 us: body(): seq_tokens = lax.all_gather(tokens, 'sp', axis=0, tiled=True)]
  transfers between devices with their start and end apart: 10 -> 16, of which waited for: 8 -> 10; matrix products, arithmetic and copies ran while one was open for 14% -> 32% of each run, Pallas kernels for 0% -> 0%
where the time goes in v1:
time: 1030 us
  waiting for transfers between devices  624 us (61%)
  matrix products  189 us (18%)
  local copies, waits for them, and re-layouts  77.7 us (8%)
  other arithmetic  72.8 us (7%)
  blocking collectives  23.4 us (2%)
  starting transfers between devices  18.7 us (2%)
  between operations  15.5 us (2%)
    psum x1, waiting for transfers between devices, body(): lax.psum((gain_grad, shift_grad, spread_bias, spread_units, jnp.sum(own_c...  129 us
    all_gather x1, waiting for transfers between devices, body(): seq_tokens = lax.all_gather(tokens, 'sp', axis=0, tiled=True)  108 us
    all_gather x1, waiting for transfers between devices, body(): seq_cotangent = lax.all_gather(cotangent, 'sp', axis=0, tiled=True)  76.3 us
    reduce_scatter x1, waiting for transfers between devices, body(): lax.psum_scatter(contract_rows(grad_pre, mlp_in).astype(low), 'dp', scatt...  72.7 us
    reduce_scatter x1, waiting for transfers between devices, body(): lax.psum_scatter(contract_rows(hidden, grad_out).astype(low), 'dp', scatt...  72.2 us
    reduce_scatter x1, waiting for transfers between devices, body(): lax.psum_scatter(partial_out.astype(low), 'sp', scatter_dimension=0, tile...  71 us
    dot_general x4, matrix products, contract_cols(): lax.dot_general(left, right, (((1,), (1,)), ((), ())), preferred_element_...  55.3 us
    dot_general x4, matrix products, contract_rows(): lax.dot_general(left, right, (((0,), (0,)), ((), ())), preferred_element_...  47.3 us
  transfers between devices with their start and end apart: 16, of which 10 were waited for; matrix products, arithmetic and copies ran while one was open for 32% of the time, Pallas kernels for 0%

profile of v1, /device:TPU:8, one launch (start us, length us, event | category | flops | bytes accessed | tf_op | source)
XLA Modules:
  0.0 1029.4 jit_solution(8558187859735132590)
XLA Ops:
  9.4 2.3 reshape.375
  11.9 23.4 %all_to_all.54 = bf16[64,3,4,512]{3,0,1,2:T(8,128)(2,1)S(1)} all-to-all(bf16[64,3,4,512]{3,0,1,2:T(8,128)(2,1)S(1)} %copy.98), channel_id=1, replica_groups=mesh['dp'=8,'sp'=4] {'sp'}, dimensions={2} | all-to-all | bytes 1572864 | tf_op jit(solution)/shard_map/all_to_all | solution.py:187
  39.0 5.4 all-to-all-start.1
  44.8 3.2 fusion.31
  49.2 107.7 %all-gather.7.cloned.1.call-done = bf16[1024,2048]{1,0:T(8,128)(2,1)} async-done(((bf16[256,2048]{1,0:T(8,128)(2,1)}), bf16[1024,2048]{1,0:T(8,128)(2,1)}) %all-gather.7.cloned.1.call-update) | async-done | bytes 4194320 | tf_op jit(solution)/shard_map/all_gather | solution.py:184
  156.9 3.0 convert_reduce_fusion
  161.6 76.3 %all-gather.17.cloned.1.call-done = bf16[1024,2048]{1,0:T(8,128)(2,1)} async-done(((bf16[256,2048]{1,0:T(8,128)(2,1)}), bf16[1024,2048]{1,0:T(8,128)(2,1)}) %all-gather.17.cloned.1.call-update) | async-done | bytes 4194320 | tf_op jit(solution)/shard_map/all_gather | solution.py:185
  237.9 4.5 broadcast_select_fusion
  245.4 3.3 convolution_convert_fusion.4
  248.7 38.2 %all-gather.13.cloned.1.call-done = bf16[2048,1536]{1,0:T(8,128)(2,1)} async-done(((bf16[256,1536]{1,0:T(8,128)(2,1)}), bf16[2048,1536]{1,0:T(8,128)(2,1)}) %all-gather.13.cloned.1.call-update) | async-done | bytes 6291472 | tf_op jit(solution)/shard_map/all_gather | solution.py:194
  287.0 11.0 %convolution_add_fusion = f32[1024,1536]{1,0:T(8,128)S(1)} fusion(bf16[2048,1536]{1,0:T(8,128)(2,1)} %all-gather.13.cloned.1.call-done, f32[1536]{0:T(1024)S(1)} %reshape.390, bf16[1024,2048]{1,0:T(8,128)(2,1)} %all-gather.7.cloned.1.call-done, f32[2048]{0:T(1024)S(1)} %bitcast.193, f32[2048]{0:T(1024)S(1)} %bitcast.190, f32[1024]{0:T(1024)S(1)} %add_rsqrt_fusion, ...), kind=kOutput, calls=%fused_computation.62 | convolution fusion | flops 6456606720 | bytes 16807936 | tf_op jit(solution)/shard_map/dot_general | solution.py:231
  298.0 2.4 fusion.36
  300.6 2.9 reshape.378
  303.6 3.7 reshape.379
  307.3 2.9 slice.122
  310.2 2.2 slice.123
  312.4 4.1 subtract_convert_fusion.2
  316.4 3.7 pad_maximum_fusion.2
  321.2 2.5 copy.106
  323.7 4.7 pad_maximum_fusion.1
  328.4 2.5 copy.119
  333.5 25.5 %while.27 = (s32[]{:T(128)}, bf16[2,512,512]{2,1,0:T(8,128)(2,1)}, f32[2,2,512]{2,1,0:T(2,128)S(1)}, s32[2]{0:T(128)S(1)}, s32[]{:T(128)}, /*index=5*/bf16[1024,...) while((s32[]{:T(128)}, bf16[2,512,512]{2,1,0:T(8,128)(2,1)}, ...), condition=%wide.region_5.6_spmd, body=%wide.region_2.5_spmd.sunk | while | flops 1087635968 | bytes 25205448 | solution.py:97
  339.5 2.8 fusion.95
  352.0 3.0 fusion.95
  359.0 51.3 %while.28 = (s32[]{:T(128)}, f32[1024,2,256]{0,2,1:T(8,128)}, f32[1024,2,256]{0,2,1:T(8,128)}, bf16[2,512,512]{1,2,0:T(8,128)(2,1)}, s32[2]{0:T(128)S(1)}, /*ind...) while((s32[]{:T(128)}, f32[1024,2,256]{0,2,1:T(8,128)}, ...), condition=%wide.region_9.10_spmd.clone, body=%wide.region_7.9_spmd.clone.sunk | while | flops 2704278016 | bytes 110660064 | solution.py:149
  363.1 4.0 fusion.108
  369.2 4.2 multiply_reduce_fusion.4
  380.0 3.0 bitcast_add_fusion.5
  387.0 4.0 fusion.108
  393.1 4.2 multiply_reduce_fusion.4
  398.7 3.8 bitcast_add_fusion.4
  405.6 4.6 bitcast_add_fusion.5
  410.3 2.3 copy.109
  416.3 2.5 slice.98
  422.3 3.3 subtract_convert_fusion.1
  425.7 7.3 pad_maximum_fusion.3
  433.6 3.1 convert_element_type.239
  438.2 13.6 %convolution_convert_fusion.2 = bf16[2048,1536]{1,0:T(8,128)(2,1)} fusion(bf16[1024,512]{1,0:T(8,128)(2,1)S(1)} %copy.111, bf16[1024,512]{1,0:T(8,128)(2,1)S(1)} %bitcast.164, bf16[1024,512]{1,0:T(8,128)(2,1)S(1)} %bitcast.161, bf16[1024,2048]{1,0:T(8,128)(2,1)} %all-gather.7.cloned.1.call-done, f32[2048]{0:T(1024)S(1)} %bitcast.194, ...), kind=kOutput, calls=%fused_computation.60 | convolution fusion | flops 6467616768 | bytes 13656064 | tf_op jit(solution)/shard_map/dot_general | solution.py:19
  453.1 4.6 convolution_convert_fusion.3
  459.2 5.1 all-to-all-start.3
  464.3 18.0 %multiply_convert_fusion.1 = (bf16[1024,2048]{1,0:T(8,128)(2,1)}, f32[1024,2048]{1,0:T(8,128)}) fusion(f32[2048]{0:T(1024)S(1)} %bitcast.183, bf16[2048,2048]{1,0:T(8,128)(2,1)} %all-gather.9.cloned.1.call-done, bf16[1024,2048]{1,0:T(8,128)(2,1)} %all-gather.7.cloned.1.call-done, f32[2048]{0:T(1024)S(1)} %bitcast.188, f32[2048]{0:T(1024)S(1)} %bitcast.185, ...), kind=kOutput, calls=%fused_computation.55 | convolution fusion | flops 8615100416 | bytes 25198592 | tf_op jit(solution)/shard_map/dot_general | solution.py:25
  482.3 17.8 %convert_reduce_fusion.1 = (f32[2048]{0:T(1024)S(1)}, bf16[1024,2048]{1,0:T(8,128)(2,1)}) fusion(f32[1024,2048]{1,0:T(8,128)} %get-tuple-element.330, f32[2048]{0:T(1024)S(1)} %bitcast.184, bf16[1024,2048]{1,0:T(8,128)(2,1)} %broadcast_select_fusion, bf16[2048,2048]{1,0:T(8,128)(2,1)} %all-gather.11.cloned.1.call-done), kind=kOutput, calls=%fused_computation.49 | convolution fusion | flops 8617195520 | bytes 25182208 | tf_op jit(solution)/shard_map/dot_general | solution.py:25
  500.1 9.6 all-to-all-done.3
  511.1 15.0 %fusion.41 = f32[1024,2048]{1,0:T(8,128)} fusion(bf16[1024,2048]{1,0:T(8,128)(2,1)} %get-tuple-element.332, bf16[2048,2048]{1,0:T(8,128)(2,1)} %all-gather.9.cloned.1.call-done), kind=kOutput, calls=%fused_computation.118 | convolution fusion | flops 8589934592 | bytes 20971520 | tf_op jit(solution)/shard_map/dot_general | solution.py:269
  526.1 16.2 %fusion.34 = (f32[2048]{0:T(1024)S(1)}, f32[2048]{0:T(1024)S(1)}, bf16[1024,2048]{1,0:T(8,128)(2,1)}, f32[2048]{0:T(1024)S(1)}, f32[2048]{0:T(1024)S(1)}, /*index=5*/f32[1024,2048]{1,0:T(8,128)}) fusion(f32[1024]{0:T(1024)S(1)} %copy-done.43, f32[1024]{0:T(1024)S(1)} %copy-done.35, bf16[1024,2048]{1,0:T(8,128)(2,1)} %all-gather.7.cloned.1.call-done, ...), kind=kOutput, calls=%fused_computation.111 | convolution fusion | flops 6479142912 | bytes 34660352 | tf_op jit(solution)/shard_map/dot_general | solution.py:25
  542.3 12.7 %fusion.40 = f32[1024,2048]{1,0:T(8,128)S(1)} fusion(bf16[1024,2048]{1,0:T(8,128)(2,1)} %get-tuple-element.329, bf16[2048,2048]{1,0:T(8,128)(2,1)} %all-gather.11.cloned.1.call-done), kind=kOutput, calls=%fused_computation.117 | convolution fusion | flops 8589934592 | bytes 20971520 | tf_op jit(solution)/shard_map/dot_general | solution.py:251
  555.0 4.4 add_convert_fusion.1
  559.5 15.0 %convolution_convert_fusion.1 = bf16[2048,2048]{1,0:T(8,128)(2,1)} fusion(bf16[1024,2048]{1,0:T(8,128)(2,1)} %get-tuple-element.332, bf16[1024,2048]{1,0:T(8,128)(2,1)} %all-gather.7.cloned.1.call-done, f32[2048]{0:T(1024)S(1)} %bitcast.189, f32[2048]{0:T(1024)S(1)} %bitcast.187, f32[1024]{0:T(1024)S(1)} %copy-done.43, f32[1024]{0:T(1024)S(1)} %copy-done.35), kind=kOutput, calls=%fused_computation.59 | convolution fusion | flops 8606711808 | bytes 16801792 | tf_op jit(solution)/shard_map/dot_general | solution.py:19
  574.5 14.1 %convolution_convert_fusion = bf16[2048,2048]{1,0:T(8,128)(2,1)} fusion(bf16[1024,2048]{1,0:T(8,128)(2,1)} %get-tuple-element.329, bf16[1024,2048]{1,0:T(8,128)(2,1)} %broadcast_select_fusion), kind=kOutput, calls=%fused_computation.58 | convolution fusion | flops 8594128896 | bytes 16777216 | tf_op jit(solution)/shard_map/dot_general | solution.py:19
  588.7 3.6 reshape.384
  592.3 2.3 copy.112
  594.6 7.6 all-to-all-start.2
  607.5 32.2 %all-to-all-done.2 = bf16[4,64,3,1,512]{4,1,3,2,0:T(8,128)(2,1)} async-done(((bf16[4,64,3,1,512]{4,1,3,2,0:T(8,128)(2,1)}), bf16[4,64,3,1,512]{4,1,3,2,0:T(8,128)(2,1)}, u32[]{:S(2)}, u32[]{:S(2)}) %all-to-all-start.2) | async-done | bytes 786464 | tf_op jit(solution)/shard_map/all_to_all | solution.py:307
  642.0 2.2 reshape.391
  644.2 11.1 %reduce-scatter.9.cloned.1.call-done = bf16[256,2048]{1,0:T(8,128)(2,1)} async-done(((bf16[1024,2048]{1,0:T(8,128)(2,1)}), bf16[256,2048]{1,0:T(8,128)(2,1)}) %reduce-scatter.9.cloned.1.call-update) | async-done | bytes 1048592 | tf_op jit(solution)/shard_map/reduce_scatter | solution.py:301
  655.3 2.5 convert_reduce_fusion.3
  657.8 4.6 convert_reduce_fusion.4
  662.4 71.0 %reduce-scatter.7.cloned.1.call-done = bf16[256,2048]{1,0:T(8,128)(2,1)} async-done(((bf16[1024,2048]{1,0:T(8,128)(2,1)}), bf16[256,2048]{1,0:T(8,128)(2,1)}) %reduce-scatter.7.cloned.1.call-update) | async-done | bytes 1048592 | tf_op jit(solution)/shard_map/reduce_scatter | solution.py:254
  733.4 2.6 add_convert_fusion.4
  736.0 72.7 %reduce-scatter.15.cloned.1.call-done = bf16[256,2048]{1,0:T(8,128)(2,1)} async-done(((bf16[2048,2048]{1,0:T(8,128)(2,1)}), bf16[256,2048]{1,0:T(8,128)(2,1)}) %reduce-scatter.15.cloned.1.call-update) | async-done | bytes 1048592 | tf_op jit(solution)/shard_map/reduce_scatter | solution.py:266
  808.7 2.8 convert_element_type.254
  811.5 72.2 %reduce-scatter.17.cloned.1.call-done = bf16[256,2048]{1,0:T(8,128)(2,1)} async-done(((bf16[2048,2048]{1,0:T(8,128)(2,1)}), bf16[256,2048]{1,0:T(8,128)(2,1)}) %reduce-scatter.17.cloned.1.call-update) | async-done | bytes 1048592 | tf_op jit(solution)/shard_map/reduce_scatter | solution.py:263
  883.7 2.8 convert_element_type.257
  886.5 129.4 %all-reduce.3.cloned.1.call-done = (f32[2,2048]{1,0:T(2,128)}, f32[2,2048]{1,0:T(2,128)}, f32[3,2048]{1,0:T(4,128)}, f32[8192]{0:T(1024)}, f32[2048]{0:T(1024)}) async-done(((f32[2,2048]{1,0:T(2,128)}, f32[2,2048]{1,0:T(2,128)}, f32[3,2048]{1,0:T(4,128)}, f32[8192]{0:T(1024)}, f32[2048]{0:T(1024)}), (f32[2,2048]{1,0:T(2,128)}, f32[2,2048]{1,0:T(2,128)}, f32[3,2048]{1,0:T(4,128)}, f32[8192]{0:T(1024)}, ...) | async-done | bytes 98320 | tf_op jit(solution)/shard_map/psum | solution.py:332
  (247 shorter events, 78.0 us)
Async XLA Ops:
  7.2 31.9 %all-gather.15.cloned.1.call-start = ((), (), s32[]{:S(2)}) async-start(), calls=%async_computation.14 | async-start | bytes 2359296 | tf_op jit(solution)/shard_map/all_gather | solution.py:199
  7.9 149.0 %all-gather.7.cloned.1.call-start = ((), (), s32[]{:S(2)}) async-start(), calls=%async_computation.10 | async-start | bytes 5242880 | tf_op jit(solution)/shard_map/all_gather | solution.py:184
  8.7 229.3 %all-gather.17.cloned.1.call-start = ((), (), s32[]{:S(2)}) async-start(), calls=%async_computation.16 | async-start | bytes 5242880 | tf_op jit(solution)/shard_map/all_gather | solution.py:185
  9.4 277.6 %all-gather.13.cloned.1.call-start = ((), (), s32[]{:S(2)}) async-start(), calls=%async_computation.13 | async-start | bytes 7077888 | tf_op jit(solution)/shard_map/all_gather | solution.py:194
  36.0 8.7 copy-start.32
  37.1 10.8 %copy-start.30 = (bf16[2,2048]{1,0:T(2,128)(2,1)S(1)}, bf16[2,2048]{1,0:T(2,128)(2,1)}, u32[]{:S(2)}) copy-start(bf16[2,2048]{1,0:T(2,128)(2,1)} %param.19) | copy-start | bytes 24580
  37.1 11.4 %copy-start.31 = (bf16[2,2048]{1,0:T(2,128)(2,1)S(1)}, bf16[2,2048]{1,0:T(2,128)(2,1)}, u32[]{:S(2)}) copy-start(bf16[2,2048]{1,0:T(2,128)(2,1)} %param.20) | copy-start | bytes 24580
  37.2 427.1 %all-gather.9.cloned.1.call-start = ((), (), s32[]{:S(2)}) async-start(), calls=%async_computation.11 | async-start | bytes 9437184 | tf_op jit(solution)/shard_map/all_gather | solution.py:197
  37.8 444.5 %all-gather.11.cloned.1.call-start = ((), (), s32[]{:S(2)}) async-start(), calls=%async_computation.12 | async-start | bytes 9437184 | tf_op jit(solution)/shard_map/all_gather | solution.py:198
  39.0 203.4 %all-to-all-start.1 = ((bf16[4,2,64,2048]{3,2,1,0:T(8,128)(2,1)}), bf16[4,2,64,2048]{3,2,1,0:T(8,128)(2,1)S(1)}, u32[]{:S(2)}, u32[]{:S(2)}) async-start(bf16[4,2,64,2048]{3,2,1,0:T(8,128)(2,1)} %bitcast.175), calls=%async_computation.1 | async-start | bytes 4194304 | tf_op jit(solution)/shard_map/all_to_all | solution.py:201
  44.4 544.3 %reduce-scatter.11.cloned.1.call-start = ((), (), s32[]{:S(2)}) async-start(), calls=%async_computation.18 | async-start | bytes 7077888 | tf_op jit(solution)/shard_map/reduce_scatter | solution.py:304
  48.6 238.4 %copy-start.38 = (f32[1,2048]{1,0:T(1,128)}, f32[1,2048]{1,0:T(1,128)S(1)}, u32[]{:S(2)}) copy-start(f32[1,2048]{1,0:T(1,128)S(1)} %get-tuple-element.322) | copy-start | bytes 24580
  49.2 237.8 %copy-start.40 = (f32[1,2048]{1,0:T(1,128)}, f32[1,2048]{1,0:T(1,128)S(1)}, u32[]{:S(2)}) copy-start(f32[1,2048]{1,0:T(1,128)S(1)} %get-tuple-element.324) | copy-start | bytes 24580
  156.9 3.4 copy-start.7
  160.4 126.6 %copy-start.34 = (f32[1024]{0:T(1024)}, f32[1024]{0:T(1024)S(1)}, u32[]{:S(2)}) copy-start(f32[1024]{0:T(1024)S(1)} %broadcast_multiply_fusion) | copy-start | bytes 12292
  161.6 125.4 %copy-start.42 = (f32[1024]{0:T(1024)}, f32[1024]{0:T(1024)S(1)}, u32[]{:S(2)}) copy-start(f32[1024]{0:T(1024)S(1)} %add_rsqrt_fusion) | copy-start | bytes 12292
  242.4 2.9 copy-start.12
  300.6 30.3 %copy-start.9 = (bf16[1024,512]{1,0:T(8,128)(2,1)}, bf16[1024,512]{1,0:T(8,128)(2,1)S(1)}, u32[]{:S(2)}) copy-start(bf16[1024,512]{1,0:T(8,128)(2,1)S(1)} %slice.121) | copy-start | bytes 3145732
  307.3 5.1 copy-start.8
  307.3 5.1 copy-start.14
  307.3 5.1 copy-start.24
  316.4 7.3 copy-start.21
  339.5 4.1 copy-start.29
  351.9 4.2 copy-start.29
  359.0 10.1 copy-start.5
  361.6 5.5 copy-start.13
  367.4 6.0 copy-start.3
  369.2 4.2 copy-start
  374.7 4.2 copy-start.27
  376.8 3.2 copy-start.1
  376.8 3.2 copy-start.4
  380.0 3.0 copy-start.6
  383.0 10.1 copy-start.5
  385.6 5.4 copy-start.13
  391.3 6.0 copy-start.3
  393.1 4.2 copy-start
  398.7 5.9 copy-start.27
  402.4 3.2 copy-start.1
  402.4 3.2 copy-start.4
  405.6 4.6 copy-start.6
  412.6 6.2 copy-start.2
  422.3 3.4 copy-start.22
  433.3 4.9 copy-start.35
  433.3 4.9 copy-start.39
  433.3 4.9 copy-start.41
  433.3 4.9 copy-start.43
  433.6 18.3 %copy-start.17 = (bf16[128,8,2,256]{3,1,2,0:T(8,128)(2,1)}, bf16[128,8,2,256]{3,1,2,0:T(8,128)(2,1)S(1)}, u32[]{:S(2)}) copy-start(bf16[128,8,2,256]{3,1,2,0:T(8,128)(2,1)S(1)} %copy.126) | copy-start | bytes 3145732
  438.2 13.7 %copy-start.19 = (bf16[1024,512]{1,0:T(8,128)(2,1)}, bf16[1024,512]{1,0:T(8,128)(2,1)S(1)}, u32[]{:S(2)}) copy-start(bf16[1024,512]{1,0:T(8,128)(2,1)S(1)} %copy.111) | copy-start | bytes 3145732
  457.7 6.6 copy-start.36
  457.7 6.6 copy-start.37
  459.2 50.5 %all-to-all-start.3 = ((bf16[2,4,64,2048]{3,2,0,1:T(8,128)(2,1)}), bf16[2,4,64,2048]{3,2,0,1:T(8,128)(2,1)S(1)}, u32[]{:S(2)}, u32[]{:S(2)}) async-start(bf16[2,4,64,2048]{3,2,0,1:T(8,128)(2,1)} %copy.114), calls=%async_computation.6 | async-start | bytes 4194304 | tf_op jit(solution)/shard_map/all_to_all | solution.py:273
  464.3 141.4 %reduce-scatter.13.cloned.1.call-start = ((), (), s32[]{:S(2)}) async-start(), calls=%async_computation.19 | async-start | bytes 2359296 | tf_op jit(solution)/shard_map/reduce_scatter | solution.py:280
  511.0 144.2 %reduce-scatter.9.cloned.1.call-start = ((), (), s32[]{:S(2)}) async-start(), calls=%async_computation.17 | async-start | bytes 5242880 | tf_op jit(solution)/shard_map/reduce_scatter | solution.py:301
  511.1 15.0 %copy-start.18 = (bf16[128,8,2,256]{3,1,2,0:T(8,128)(2,1)S(1)}, bf16[128,8,2,256]{3,1,2,0:T(8,128)(2,1)}, u32[]{:S(2)}) copy-start(bf16[128,8,2,256]{3,1,2,0:T(8,128)(2,1)} %copy-done.17) | copy-start | bytes 3145732
  511.1 15.0 %copy-start.20 = (bf16[1024,512]{1,0:T(8,128)(2,1)S(1)}, bf16[1024,512]{1,0:T(8,128)(2,1)}, u32[]{:S(2)}) copy-start(bf16[1024,512]{1,0:T(8,128)(2,1)} %copy-done.19) | copy-start | bytes 3145732
  542.2 191.1 %reduce-scatter.7.cloned.1.call-start = ((), (), s32[]{:S(2)}) async-start(), calls=%async_computation.15 | async-start | bytes 5242880 | tf_op jit(solution)/shard_map/reduce_scatter | solution.py:254
  542.3 12.7 %copy-start.26 = (bf16[1,2,4,64,2048]{4,3,2,1,0:T(8,128)(2,1)S(1)}, bf16[1,2,4,64,2048]{4,3,2,1,0:T(8,128)(2,1)}, u32[]{:S(2)}) copy-start(bf16[1,2,4,64,2048]{4,3,2,1,0:T(8,128)(2,1)} %copy-done.25) | copy-start | bytes 6291460
  542.3 12.7 %copy-start.46 = (bf16[2,512,512]{2,1,0:T(8,128)(2,1)S(1)}, bf16[2,512,512]{2,1,0:T(8,128)(2,1)}, u32[]{:S(2)}) copy-start(bf16[2,512,512]{2,1,0:T(8,128)(2,1)} %get-tuple-element.113) | copy-start | bytes 3145732
  559.4 249.2 %reduce-scatter.15.cloned.1.call-start = ((), (), s32[]{:S(2)}) async-start(), calls=%async_computation.20 | async-start | bytes 9437184 | tf_op jit(solution)/shard_map/reduce_scatter | solution.py:266
  574.5 309.2 %reduce-scatter.17.cloned.1.call-start = ((), (), s32[]{:S(2)}) async-start(), calls=%async_computation.21 | async-start | bytes 9437184 | tf_op jit(solution)/shard_map/reduce_scatter | solution.py:263
  588.7 13.5 %copy-start.44 = (bf16[2048]{0:T(1024)(128)(2,1)S(1)}, bf16[2048]{0:T(1024)(128)(2,1)}, u32[]{:S(2)}) copy-start(bf16[2048]{0:T(1024)(128)(2,1)} %param.27) | copy-start | bytes 12292
  594.6 45.1 %all-to-all-start.2 = ((bf16[4,64,3,1,512]{4,1,3,2,0:T(8,128)(2,1)}), bf16[4,64,3,1,512]{4,1,3,2,0:T(8,128)(2,1)}, u32[]{:S(2)}, u32[]{:S(2)}) async-start(bf16[4,64,3,1,512]{4,1,3,2,0:T(8,128)(2,1)} %copy.112), calls=%async_computation.5 | async-start | bytes 1572864 | tf_op jit(solution)/shard_map/all_to_all | solution.py:307
  602.1 413.8 %all-reduce.3.cloned.1.call-start = ((), (), s32[]{:S(2)}) async-start(), calls=%async_computation.22 | async-start | bytes 212992 | tf_op jit(solution)/shard_map/psum | solution.py:332
  655.3 78.1 %copy-start.16 = (bf16[256,2048]{1,0:T(8,128)(2,1)S(1)}, bf16[256,2048]{1,0:T(8,128)(2,1)}, u32[]{:S(2)}) copy-start(bf16[256,2048]{1,0:T(8,128)(2,1)} %param.16) | copy-start | bytes 3145732
  (9 other events, 13.6 us)
Sparse Core Ops, SparseCore 0:
  9.9 29.0 all-gather.14
  40.6 116.3 all-gather.6
  158.5 79.3 all-gather.16
  240.2 46.6 all-gather.12
  288.7 54.3 all-gather.8
  344.9 54.3 all-gather.10
  452.0 61.7 reduce-scatter.10
  518.1 41.2 reduce-scatter.12
  561.6 93.5 reduce-scatter.8
  657.5 75.8 reduce-scatter.6
  736.8 71.7 reduce-scatter.14
  812.4 71.2 reduce-scatter.16
  891.3 124.5 all-reduce.2

commit v2 on v1

v2 whole, which is shorter than its diff:
```python
import functools

import jax
import jax.numpy as jnp
from jax import lax
from jax.experimental import pallas as pl
from jax.experimental.pallas import tpu as pltpu
from jax.sharding import PartitionSpec as P

D = 2048
HEADS = 8
HEAD = 256
ROT = 64


eps = 1e-05
base_freq = 10000.0
root_half = 0.7071067811865476
inv_root_two_pi = 0.3989422804014327


def contract_rows(left, right):
    return lax.dot_general(
        left, right, (((0,), (0,)), ((), ())), preferred_element_type=jnp.float32
    )


def contract_cols(left, right):
    return lax.dot_general(
        left, right, (((1,), (1,)), ((), ())), preferred_element_type=jnp.float32
    )


def gelu_value(pre_act):
    return 0.5 * pre_act * (1.0 + lax.erf(pre_act * root_half))


def gelu_slope(pre_act):
    return 0.5 * (1.0 + lax.erf(pre_act * root_half)) + pre_act * inv_root_two_pi * jnp.exp(
        -0.5 * pre_act * pre_act
    )


BAND=256
def turn(x, cos_t, sin_t):
    first = x[:, :128]
    lane = lax.broadcasted_iota(jnp.int32, first.shape, 1)
    partner = jnp.where(lane < ROT // 2, pltpu.roll(first, 128 - ROT // 2, 1), pltpu.roll(first, ROT // 2, 1))
    return jnp.concatenate([first * cos_t + partner * sin_t, x[:, 128:]], axis=1)

def weights_of(q, k, start, length, scale):
    rows, cols = q.shape[0], k.shape[0]
    s = lax.dot_general(q, k, (((1,), (1,)), ((), ())), preferred_element_type=jnp.float32) * scale
    key = lax.broadcasted_iota(jnp.int32, (rows, cols), 1)
    query = start + lax.broadcasted_iota(jnp.int32, (rows, cols), 0)
    s = jnp.where((key <= query) & (key < length), s, -1e30)
    e = jnp.exp(s - jnp.max(s, axis=-1, keepdims=True))
    return e / jnp.sum(e, axis=-1, keepdims=True)

def fwd_kernel(scale, len_ref, pq, pk, pv, bq, bk, bv, cos_ref, sin_ref, q_ref, k_ref, v_ref, ctx_ref):
    length = len_ref[0]
    seq = pq.shape[0]
    cos_t, sin_t = cos_ref[...], sin_ref[...]
    q_ref[...] = turn(pq[...] + bq[...], cos_t, sin_t).astype(jnp.bfloat16)
    k_ref[...] = turn(pk[...] + bk[...], cos_t, sin_t).astype(jnp.bfloat16)
    v_ref[...] = (pv[...] + bv[...]).astype(jnp.bfloat16)
    for start in range(0, seq, BAND):
        end = start + BAND
        p = weights_of(q_ref[start:end, :], k_ref[:end, :], start, length, scale)
        ctx_ref[start:end, :] = jnp.dot(p.astype(jnp.bfloat16), v_ref[:end, :], preferred_element_type=jnp.float32).astype(jnp.bfloat16)

def attend_fwd(projected, bias, cos_t, sin_t, lengths):
    seq, width = projected.shape
    heads = width // 3 // HEAD
    col = lambda g: pl.BlockSpec((seq, HEAD), lambda h, *_, g=g: (0, g * heads + h))
    bcol = lambda g: pl.BlockSpec((1, HEAD), lambda h, *_, g=g: (0, g * heads + h))
    tab = pl.BlockSpec((seq, 128), lambda h, *_: (0, 0))
    out = pl.BlockSpec((seq, HEAD), lambda h, *_: (0, h))
    return pl.pallas_call(
        functools.partial(fwd_kernel, HEAD ** -0.5),
        grid_spec=pltpu.PrefetchScalarGridSpec(num_scalar_prefetch=1, grid=(heads,),
            in_specs=[col(0), col(1), col(2), bcol(0), bcol(1), bcol(2), tab, tab], out_specs=[out] * 4),
        out_shape=[jax.ShapeDtypeStruct((seq, heads * HEAD), jnp.bfloat16)] * 4,
        name="attend_fwd",
        cost_estimate=pl.CostEstimate(flops=heads * seq * seq * HEAD * 4, bytes_accessed=seq * width * 8, transcendentals=heads * seq * seq),
    )(lengths, projected, projected, projected, bias, bias, bias, cos_t, sin_t)

def bwd_kernel(scale, heads, len_ref, q_ref, k_ref, v_ref, g_ref, cos_ref, sin_ref, gp_ref, sum_ref, dk, dv, dq):
    length = len_ref[0]
    h = pl.program_id(0)
    seq = q_ref.shape[0]
    dk[...] = jnp.zeros_like(dk)
    dv[...] = jnp.zeros_like(dv)
    for start in range(0, seq, BAND):
        end = start + BAND
        q, g = q_ref[start:end, :], g_ref[start:end, :]
        k, v = k_ref[:end, :], v_ref[:end, :]
        p = weights_of(q, k, start, length, scale)
        gp = lax.dot_general(g, v, (((1,), (1,)), ((), ())), preferred_element_type=jnp.float32)
        ds = (p * (gp - jnp.sum(p * gp, axis=-1, keepdims=True))).astype(jnp.bfloat16)
        dq[start:end, :] = jnp.dot(ds, k, preferred_element_type=jnp.float32) * scale
        dk[:end, :] += lax.dot_general(ds, q, (((0,), (0,)), ((), ())), preferred_element_type=jnp.float32)
        dv[:end, :] += lax.dot_general(p.astype(jnp.bfloat16), g, (((0,), (0,)), ((), ())), preferred_element_type=jnp.float32)
    cos_t, sin_t = cos_ref[...], sin_ref[...]
    def back(x):
        return turn(x.astype(jnp.bfloat16).astype(jnp.float32), cos_t, -sin_t).astype(jnp.bfloat16)
    for g, piece in enumerate((back(dq[...]), back(dk[...] * scale), dv[...].astype(jnp.bfloat16))):
        at = pl.ds(pl.multiple_of((g * heads + h) * HEAD, HEAD), HEAD)
        gp_ref[:, at] = piece
        sum_ref[:, at] = jnp.sum(piece.astype(jnp.float32), axis=0, keepdims=True)

def attend_bwd(q, k, v, gctx, cos_t, sin_t, lengths):
    seq, width = q.shape
    heads = width // HEAD
    col = pl.BlockSpec((seq, HEAD), lambda h, *_: (0, h))
    tab = pl.BlockSpec((seq, 128), lambda h, *_: (0, 0))
    return pl.pallas_call(
        functools.partial(bwd_kernel, HEAD ** -0.5, heads),
        grid_spec=pltpu.PrefetchScalarGridSpec(num_scalar_prefetch=1, grid=(heads,),
            in_specs=[col] * 4 + [tab, tab],
            out_specs=[pl.BlockSpec((seq, 3 * width), lambda h, *_: (0, 0)), pl.BlockSpec((1, 3 * width), lambda h, *_: (0, 0))],
            scratch_shapes=[pltpu.VMEM((seq, HEAD), jnp.float32)] * 3),
        out_shape=[jax.ShapeDtypeStruct((seq, 3 * width), jnp.bfloat16), jax.ShapeDtypeStruct((1, 3 * width), jnp.float32)],
        name="attend_bwd",
        cost_estimate=pl.CostEstimate(flops=heads * seq * seq * HEAD * 10, bytes_accessed=seq * width * 20, transcendentals=heads * seq * seq),
    )(lengths, q, k, v, gctx, cos_t, sin_t)

def rotary_rows(seq):
    half = ROT // 2
    freq = 10000.0 ** (-jnp.arange(half, dtype=jnp.float32) * (2.0 / ROT))
    ang = jnp.arange(seq, dtype=jnp.int32).astype(jnp.float32)[:, None] * freq[None, :]
    c, s = jnp.cos(ang), jnp.sin(ang)
    rest = 128 - ROT
    return (jnp.concatenate([c, c, jnp.ones((seq, rest), jnp.float32)], 1), jnp.concatenate([-s, s, jnp.zeros((seq, rest), jnp.float32)], 1))

MESH = pl.DeviceIdType.MESH

def square_partners(dp):
    core, x, y = dp % 2, (dp // 2) % 2, dp // 4
    across_x, across_y = dp + 2 - 4 * x, dp + 4 - 8 * y
    first = across_x * (1 - core) + across_y * core
    second = across_y * (1 - core) + across_x * core
    return first, second, across_x + across_y - dp, 1 - 2 * core

def gather_kernel(sp_size, qkv_ref, out_ref, up_ref, down_ref, qkv_all, out_all, up_all, down_all,
                  send_sem, recv_sem, slab_send, slab_recv, local_sem, turn_send, turn_recv):
    dp, sp = lax.axis_index("dp"), lax.axis_index("sp")
    first, second, diagonal, flip = square_partners(dp)
    sibling = dp + flip
    per = 2
    pair, lane = dp // per, dp % per
    rows = qkv_ref.shape[0]
    wide = up_ref.shape[1]
    head_width = wide // sp_size
    turn_dp = sp * per + lane

    barrier = pltpu.get_barrier_semaphore()
    for other in (first, second, sibling):
        pl.semaphore_signal(barrier, inc=1, device_id=(other, sp), device_id_type=MESH)
    for step in range(1, sp_size):
        pl.semaphore_signal(barrier, inc=1, device_id=(dp, lax.rem(sp + step, sp_size)), device_id_type=MESH)
    @pl.when(pair != sp)
    def _():
        pl.semaphore_signal(barrier, inc=1, device_id=(turn_dp, pair), device_id_type=MESH)

    pl.semaphore_wait(barrier, 2 + sp_size + jnp.where(pair != sp, 1, 0))

    def slab_at(owner_sp):
        return pl.ds(pl.multiple_of((dp * sp_size + owner_sp) * rows, rows), rows)

    def slab_copy(step, part):
        there = lax.rem(sp + step, sp_size)
        return pltpu.make_async_remote_copy(
            src_ref=qkv_ref.at[:, pl.ds(pl.multiple_of(part * wide + there * head_width, head_width), head_width)],
            dst_ref=qkv_all.at[slab_at(sp), pl.ds(part * head_width, head_width)],
            send_sem=slab_send.at[step - 1, part], recv_sem=slab_recv.at[step - 1, part],
            device_id=(dp, there), device_id_type=MESH)

    def slab_arrival(step, part):
        origin = lax.rem(sp + sp_size - step, sp_size)
        return pltpu.make_async_remote_copy(
            src_ref=qkv_ref.at[:, pl.ds(part * head_width, head_width)],
            dst_ref=qkv_all.at[slab_at(origin), pl.ds(part * head_width, head_width)],
            send_sem=slab_send.at[step - 1, part], recv_sem=slab_recv.at[step - 1, part],
            device_id=(dp, origin), device_id_type=MESH)

    units = up_ref.shape[0]
    slab = rows * sp_size

    def plain(height):
        return lambda owner: pl.ds(pl.multiple_of(owner * height, height), height)

    def turned(owner):
        return pl.ds(pl.multiple_of((owner % per) * slab + (owner // per) * rows, rows), rows)

    arrays = ((up_ref, up_all, plain(units)), (down_ref, down_all, plain(units)), (None, qkv_all, plain(slab)), (None, out_all, turned))

    def copy(index, message, block, target):
        source, result, place = arrays[index]
        at = result.at[place(block)]
        src = at
        if source is not None and message < 3:
            src = source
        return pltpu.make_async_remote_copy(
            src_ref=src, dst_ref=at, send_sem=send_sem.at[index, message], recv_sem=recv_sem.at[index, message],
            device_id=(target, sp), device_id_type=MESH)

    sends = ((dp, first), (dp, second), (dp, sibling), (first, second), (first, sibling), (second, sibling), (diagonal, sibling))
    arrivals = (first, second, sibling, diagonal, second + flip, first + flip, diagonal + flip)

    def start(index, message):
        copy(index, message, *sends[message]).start()

    def arrived(index, message):
        copy(index, message, arrivals[message], dp).wait_recv()

    def own(index):
        for message in (0, 1, 2):
            start(index, message)

    def keep(source, target, which):
        return pltpu.make_async_copy(source, target, local_sem.at[which])

    own(0)
    for step in range(1, sp_size):
        for part in range(3):
            slab_copy(step, part).start()

    out_place = out_all.at[turned(turn_dp)]
    my_out_place = out_all.at[turned(dp)]
    turn = pltpu.make_async_remote_copy(
        src_ref=out_ref, dst_ref=out_place, send_sem=turn_send, recv_sem=turn_recv,
        device_id=(turn_dp, pair), device_id_type=MESH)
    turn_arrival = pltpu.make_async_remote_copy(
        src_ref=out_ref, dst_ref=my_out_place, send_sem=turn_send, recv_sem=turn_recv,
        device_id=(turn_dp, pair), device_id_type=MESH)

    @pl.when(pair != sp)
    def _():
        turn.start()

    own(1)
    local = [keep(up_ref, up_all.at[plain(units)(dp)], 0), keep(down_ref, down_all.at[plain(units)(dp)], 1)]
    for part in range(3):
        local.append(keep(
            qkv_ref.at[:, pl.ds(pl.multiple_of(part * wide + sp * head_width, head_width), head_width)],
            qkv_all.at[slab_at(sp), pl.ds(part * head_width, head_width)], 2 + part))
    for c in local:
        c.start()

    def onward(index):
        arrived(index, 0)
        start(index, 3)
        start(index, 4)
        arrived(index, 1)
        start(index, 5)

    onward(0)
    for step in range(1, sp_size):
        for part in range(3):
            slab_arrival(step, part).wait_recv()
    for c in local:
        c.wait()
    own(2)

    @pl.when(pair == sp)
    def _():
        c = keep(out_ref, my_out_place, 5)
        c.start()
        c.wait()

    @pl.when(pair != sp)
    def _():
        turn_arrival.wait_recv()

    own(3)
    onward(1)
    onward(2)
    onward(3)
    for index in range(4):
        arrived(index, 3)
        start(index, 6)
    for index in range(4):
        for message in (2, 4, 5, 6):
            arrived(index, message)
    for index in range(4):
        for message in range(7):
            copy(index, message, *sends[message]).wait_send()
    for step in range(1, sp_size):
        for part in range(3):
            slab_copy(step, part).wait_send()

    @pl.when(pair != sp)
    def _():
        turn.wait_send()

def gather_weights(dp_size, sp_size, qkv_weight, out_weight, up_weight, down_weight):
    rows, wide = out_weight.shape
    units = up_weight.shape[0]
    low = jnp.bfloat16
    hbm = pl.BlockSpec(memory_space=pltpu.HBM)
    vmem = pl.BlockSpec(memory_space=pltpu.VMEM)
    dma = pltpu.SemaphoreType.DMA
    return pl.pallas_call(
        functools.partial(gather_kernel, sp_size),
        out_shape=[jax.ShapeDtypeStruct((rows * sp_size * dp_size, 3 * wide // sp_size), low),
                   jax.ShapeDtypeStruct((rows * dp_size, wide), low),
                   jax.ShapeDtypeStruct((units * dp_size, wide), low),
                   jax.ShapeDtypeStruct((units * dp_size, wide), low)],
        in_specs=[vmem] * 4, out_specs=[hbm] * 4,
        scratch_shapes=[dma((4, 7)), dma((4, 7)), dma((sp_size - 1, 3)), dma((sp_size - 1, 3)), dma((6,)), dma, dma],
        compiler_params=pltpu.CompilerParams(collective_id=0, has_side_effects=True),
        cost_estimate=pl.CostEstimate(flops=0, bytes_accessed=300 * 1000 * 1000, transcendentals=0),
        name="gather_weights",
    )(qkv_weight, out_weight, up_weight, down_weight)

def gather_plain(dp_size, sp_size, qkv_weight, out_weight, up_weight, down_weight):
    head_width = D // sp_size
    qkv_rows = qkv_weight.shape[0]
    qkv_slab = lax.all_to_all(
        qkv_weight.reshape(qkv_rows, 3, sp_size, head_width),
        "sp",
        split_axis=2,
        concat_axis=0,
        tiled=True,
    )
    qkv_own = lax.all_gather(
        qkv_slab.reshape(qkv_rows * sp_size, 3 * head_width), "dp", axis=0, tiled=True
    )
    up_own = lax.all_gather(up_weight, "dp", axis=0, tiled=True)
    down_own = lax.all_gather(down_weight, "dp", axis=0, tiled=True)
    out_blocks = lax.all_gather(out_weight, "dp", axis=0, tiled=True)
    out_own = lax.all_to_all(
        out_blocks.reshape(sp_size, dp_size // sp_size, qkv_rows, D),
        "sp",
        split_axis=0,
        concat_axis=2,
        tiled=True,
    ).reshape(head_width, D)
    return qkv_own, out_own, up_own, down_own


def body(
    tokens,
    lengths,
    cotangent,
    ln_gains,
    ln_shifts,
    qkv_weight,
    qkv_bias,
    out_weight,
    up_weight,
    up_bias,
    down_weight,
    out_bias,
):
    dp_size = lax.axis_size("dp")
    sp_size = lax.axis_size("sp")
    shard = lax.axis_index("sp")
    own_rows = tokens.shape[0]
    seq_rows = own_rows * sp_size
    head_width = D // sp_size
    length = lengths[0]
    low = jnp.bfloat16
    full = jnp.float32

    seq_tokens = lax.all_gather(tokens, "sp", axis=0, tiled=True)
    seq_cotangent = lax.all_gather(cotangent, "sp", axis=0, tiled=True)
    qkv_rows = qkv_weight.shape[0]
    per_shard = dp_size // sp_size
    square = dp_size == 8 and sp_size == 4
    gather = gather_weights if square else gather_plain
    qkv_own, out_own, up_own, down_own = gather(
        dp_size, sp_size, qkv_weight, out_weight, up_weight, down_weight
    )
    units = up_weight.shape[0]
    unit_bias = lax.dynamic_index_in_dim(
        up_bias.reshape(dp_size, sp_size, units), shard, 1, keepdims=False
    ).reshape(dp_size * units)
    bias_own = lax.dynamic_index_in_dim(
        qkv_bias.reshape(3, sp_size, head_width), shard, 1, keepdims=False
    ).reshape(3 * head_width)

    positions = jnp.arange(seq_rows, dtype=jnp.int32)
    cos_rows, sin_rows = rotary_rows(seq_rows)
    gains = ln_gains.astype(full)
    shifts = ln_shifts.astype(full)
    inputs = seq_tokens.astype(full)
    centre = jnp.mean(inputs, axis=-1, keepdims=True)
    centered = inputs - centre
    inverse = lax.rsqrt(jnp.mean(centered * centered, axis=-1, keepdims=True) + eps)
    normed = centered * inverse
    attn_in = (normed * gains[0] + shifts[0]).astype(low)
    mlp_in = (normed * gains[1] + shifts[1]).astype(low)
    row_valid = positions < length
    grad_out = jnp.where(row_valid[:, None], seq_cotangent, jnp.zeros_like(seq_cotangent))

    projected = jnp.dot(attn_in, qkv_own, preferred_element_type=full)
    queries, key_rows, values, context = attend_fwd(
        projected, bias_own.astype(full)[None], cos_rows, sin_rows, lengths
    )

    pre_act = contract_cols(mlp_in, up_own) + unit_bias.astype(full)
    hidden = gelu_value(pre_act).astype(low)
    partial_out = jnp.dot(hidden, down_own, preferred_element_type=full) + jnp.dot(
        context, out_own, preferred_element_type=full
    )
    reduced_out = lax.psum_scatter(
        partial_out.astype(low), "sp", scatter_dimension=0, tiled=True
    )
    output = (
        tokens.astype(full) + reduced_out.astype(full) + out_bias.astype(full)
    ).astype(low)

    grad_hidden = contract_cols(grad_out, down_own)
    grad_pre = (grad_hidden * gelu_slope(pre_act)).astype(low)
    grad_down = lax.psum_scatter(
        contract_rows(hidden, grad_out).astype(low), "dp", scatter_dimension=0, tiled=True
    )
    grad_up = lax.psum_scatter(
        contract_rows(grad_pre, mlp_in).astype(low), "dp", scatter_dimension=0, tiled=True
    )
    grad_mlp_in = jnp.dot(grad_pre, up_own, preferred_element_type=full)

    grad_context = contract_cols(grad_out, out_own).astype(low)
    grad_dense = contract_rows(context, grad_out).astype(low)
    grad_dense = lax.all_to_all(
        grad_dense.reshape(per_shard, sp_size, qkv_rows, D),
        "sp",
        split_axis=1,
        concat_axis=0,
        tiled=True,
    ).reshape(dp_size * qkv_rows, D)
    grad_dense = lax.psum_scatter(grad_dense, "dp", scatter_dimension=0, tiled=True)
    grad_proj, grad_proj_sum = attend_bwd(
        queries, key_rows, values, grad_context, cos_rows, sin_rows, lengths
    )
    grad_attn_in = contract_cols(grad_proj, qkv_own)
    grad_hat = grad_attn_in * gains[0] + grad_mlp_in * gains[1]
    reduced_hat = lax.psum_scatter(
        grad_hat.astype(low), "sp", scatter_dimension=0, tiled=True
    ).astype(full)
    grad_qkv = lax.psum_scatter(
        contract_rows(attn_in, grad_proj).astype(low), "dp", scatter_dimension=0, tiled=True
    )
    grad_qkv = lax.all_to_all(
        grad_qkv.reshape(sp_size, qkv_rows, 3, 1, head_width),
        "sp",
        split_axis=0,
        concat_axis=3,
        tiled=True,
    ).reshape(qkv_rows, 3 * D)

    own_cotangent = lax.dynamic_slice_in_dim(grad_out, shard * own_rows, own_rows, 0).astype(full)
    spread_units = lax.dynamic_update_index_in_dim(
        jnp.zeros((dp_size, sp_size, units), full),
        jnp.sum(grad_pre, axis=0, dtype=full).reshape(dp_size, units),
        shard,
        1,
    ).reshape(-1)
    spread_bias = lax.dynamic_update_index_in_dim(
        jnp.zeros((3, sp_size, head_width), full),
        grad_proj_sum.reshape(3, head_width),
        shard,
        1,
    ).reshape(3, D)
    gain_grad = jnp.stack(
        [jnp.sum(grad_attn_in * normed, axis=0), jnp.sum(grad_mlp_in * normed, axis=0)]
    )
    shift_grad = jnp.stack([jnp.sum(grad_attn_in, axis=0), jnp.sum(grad_mlp_in, axis=0)])
    gain_total, shift_total, qkv_bias_total, unit_total, out_bias_total = lax.psum(
        (gain_grad, shift_grad, spread_bias, spread_units, jnp.sum(own_cotangent, axis=0)),
        ("dp", "sp"),
    )

    own_inverse = lax.dynamic_slice_in_dim(inverse, shard * own_rows, own_rows, 0)
    own_normed = lax.dynamic_slice_in_dim(normed, shard * own_rows, own_rows, 0)
    grad_input = own_inverse * (
        reduced_hat
        - jnp.mean(reduced_hat, axis=-1, keepdims=True)
        - own_normed * jnp.mean(reduced_hat * own_normed, axis=-1, keepdims=True)
    )
    input_grad = (own_cotangent + grad_input).astype(low)
    return (
        output,
        input_grad,
        gain_total,
        shift_total,
        grad_qkv.astype(full),
        qkv_bias_total,
        grad_dense.astype(full),
        grad_up.astype(full),
        unit_total,
        grad_down.astype(full),
        out_bias_total,
    )


def solution(mesh):
    return jax.shard_map(
        body,
        mesh=mesh,
        in_specs=(
            P(("dp", "sp"), None),
            P("dp"),
            P(("dp", "sp"), None),
            P(),
            P(),
            P(("dp", "sp"), None),
            P(),
            P(("dp", "sp"), None),
            P(("dp", "sp"), None),
            P(),
            P(("dp", "sp"), None),
            P(),
        ),
        out_specs=(
            P(("dp", "sp"), None),
            P(("dp", "sp"), None),
            P(),
            P(),
            P(("dp", "sp"), None),
            P(),
            P(("dp", "sp"), None),
            P(("dp", "sp"), None),
            P(),
            P(("dp", "sp"), None),
            P(),
        ),
        check_vma=False,
    )
```

time: 1030 us -> 841 us (0.82)
  waiting for transfers between devices: 624 us -> 468 us
  Pallas kernels: 0 us -> 143 us
  local copies, waits for them, and re-layouts: 77.7 us -> 24 us
  matrix products: 189 us -> 142 us
  other arithmetic: 72.8 us -> 31.2 us
  blocking collectives: 23.4 us -> 0 us
    pallas_call x0 -> x3, Pallas kernels: none -> 143 us  [the longest x1 121 us: gather_weights(): pl.pallas_call(functools.partial(gather_kernel, sp_size), out_shape=[jax....]
    all_gather x1, waiting for transfers between devices: 108 us -> 0.02 us  [body(): seq_tokens = lax.all_gather(tokens, 'sp', axis=0, tiled=True)]
    reduce_scatter x1, waiting for transfers between devices: 0.02 us -> 63.1 us  [body(): lax.psum_scatter(contract_rows(attn_in, grad_proj).astype(low), 'dp', sca...]
    all_gather x1, waiting for transfers between devices: 76.3 us -> 30.5 us  [body(): seq_cotangent = lax.all_gather(cotangent, 'sp', axis=0, tiled=True)]
    dot_general x15 -> x1, matrix products: 54.5 us -> 11.9 us  [body(): projected = jnp.dot(attn_in, qkv_own, preferred_element_type=full)]
    all_gather x4 -> x0, waiting for transfers between devices: 38.3 us -> none  [the longest x1 38.2 us: body(): lax.all_gather(qkv_slab.reshape(qkv_rows * sp_size, 3 * head_width), 'dp'...]
    all_to_all x1, waiting for transfers between devices: 32.2 us -> 0.01 us  [body(): lax.all_to_all(grad_qkv.reshape(sp_size, qkv_rows, 3, 1, head_width), 'sp...]
    all_to_all x1 -> x0, blocking collectives: 23.4 us -> none  [body(): lax.all_to_all(qkv_weight.reshape(qkv_rows, 3, sp_size, head_width), 'sp'...]
  transfers between devices with their start and end apart: 16 -> 11, of which waited for: 10 -> 7; matrix products, arithmetic and copies ran while one was open for 32% -> 21% of each run, Pallas kernels for 0% -> 17%
where the time goes in v2:
time: 841 us; the launch traced here: 835 us
  waiting for transfers between devices  468 us (56%)
  Pallas kernels  143 us (17%)
  matrix products  142 us (17%)
  other arithmetic  31.2 us (4%)
  local copies, waits for them, and re-layouts  24 us (3%)
  between operations  15.2 us (2%)
  starting transfers between devices  12.2 us (1%)
    psum x1, waiting for transfers between devices, body(): lax.psum((gain_grad, shift_grad, spread_bias, spread_units, jnp.sum(own_c...  129 us
    pallas_call x1, Pallas kernels, gather_weights(): pl.pallas_call(functools.partial(gather_kernel, sp_size), out_shape=[jax....  121 us
    reduce_scatter x1, waiting for transfers between devices, body(): lax.psum_scatter(partial_out.astype(low), 'sp', scatter_dimension=0, tile...  82.5 us
    reduce_scatter x1, waiting for transfers between devices, body(): lax.psum_scatter(contract_rows(hidden, grad_out).astype(low), 'dp', scatt...  72.4 us
    reduce_scatter x1, waiting for transfers between devices, body(): lax.psum_scatter(contract_rows(grad_pre, mlp_in).astype(low), 'dp', scatt...  67.4 us
    reduce_scatter x1, waiting for transfers between devices, body(): lax.psum_scatter(contract_rows(attn_in, grad_proj).astype(low), 'dp', sca...  63.1 us
    dot_general x4, matrix products, contract_cols(): lax.dot_general(left, right, (((1,), (1,)), ((), ())), preferred_element_...  56.1 us
    dot_general x4, matrix products, contract_rows(): lax.dot_general(left, right, (((0,), (0,)), ((), ())), preferred_element_...  43.3 us
  transfers between devices with their start and end apart: 11, of which 7 were waited for; matrix products, arithmetic and copies ran while one was open for 21% of the time, Pallas kernels for 17%

profile of v2, /device:TPU:8, one launch (start us, length us, event | category | flops | bytes accessed | tf_op | source)
XLA Modules:
  0.0 835.4 jit_solution(7442595877389082118)
XLA Ops:
  7.2 0.7 all-gather.3.cloned.1.call-update
  8.0 0.7 all-gather.5.cloned.1.call-update
  8.7 0.7 convert_bitcast_fusion.1
  9.4 0.6 copy.45
  10.0 0.1 pad.6.clone
  10.1 0.1 pad.9.clone
  10.8 0.7 reshape.127
  11.5 121.1 %gather_weights.1 = (bf16[2048,1536]{1,0:T(8,128)(2,1)}, bf16[512,2048]{1,0:T(8,128)(2,1)}, bf16[2048,2048]{1,0:T(8,128)(2,1)}, bf16[2048,2048]{1,0:T(8,128)(2,1)}) custom-call(bf16[64,6144]{1,0:T(8,128)(2,1)} %qkv_ref.1, bf16[64,2048]{1,0:T(8,128)(2,1)} %out_ref.1, bf16[256,2048]{1,0:T(8,128)(2,1)} %up_ref.1, bf16[256,2048]{1,0:T(8,128)(2,1)} %down_ref.1), custom_call_target="tpu_custom_call" | custom-call | bytes 300000000 | tf_op jit(solution)/shard_map/gather_weights/pallas_call | solution.py:304
  132.7 1.9 fusion.12
  134.6 1.3 maximum_maximum_fusion
  136.0 3.0 convert_reduce_fusion
  139.0 3.4 fusion.2
  142.4 11.9 %fusion.14.pq.pk.pv = f32[1024,1536]{1,0:T(8,128)} fusion(bf16[2048,1536]{1,0:T(8,128)(2,1)} %get-tuple-element.23, bf16[1024,2048]{1,0:T(8,128)(2,1)S(1)} %copy-done, f32[2048]{0:T(1024)S(1)} %bitcast.79, f32[2048]{0:T(1024)S(1)} %bitcast.76, f32[1024]{0:T(1024)S(1)} %add_rsqrt_fusion, f32[1024]{0:T(1024)S(1)} %broadcast_multiply_fusion), kind=kOutput, calls=%fused_computation.54 | convolution fusion | flops 6455033856 | bytes 16801792 | tf_op jit(solution)/shard_map/dot_general | solution.py:398
  154.3 9.3 %attend_fwd.1 = (bf16[1024,512]{1,0:T(8,128)(2,1)}, bf16[1024,512]{1,0:T(8,128)(2,1)}, bf16[1024,512]{1,0:T(8,128)(2,1)}, bf16[1024,512]{1,0:T(8,128)(2,1)}) custom-call(s32[1]{0:T(128)} %copy.55.len_ref, f32[1024,1536]{1,0:T(8,128)} %fusion.14.pq.pk.pv, f32[1024,1536]{1,0:T(8,128)} %fusion.14.pq.pk.pv, f32[1024,1536]{1,0:T(8,128)} %fusion.14.pq.pk.pv, ...), custom_call_target="tpu_custom_call" | custom-call | flops 2147483648 | bytes 12582912 | tf_op jit(solution)/shard_map/attend_fwd/pallas_call | solution.py:79
  163.6 30.5 %all-gather.5.cloned.1.call-done = bf16[1024,2048]{1,0:T(8,128)(2,1)} async-done(((bf16[256,2048]{1,0:T(8,128)(2,1)}), bf16[1024,2048]{1,0:T(8,128)(2,1)}) %all-gather.5.cloned.1.call-update) | async-done | bytes 4194320 | tf_op jit(solution)/shard_map/all_gather | solution.py:368
  194.0 2.5 broadcast_select_fusion
  196.6 1.9 copy-done.2
  198.5 2.5 convolution_convert_fusion.3
  201.0 1.5 copy.44
  202.4 6.8 all-to-all-start.1
  209.2 17.4 %multiply_convert_fusion = (bf16[1024,2048]{1,0:T(8,128)(2,1)}, f32[1024,2048]{1,0:T(8,128)}) fusion(f32[2048]{0:T(1024)S(1)} %bitcast.65, bf16[2048,2048]{1,0:T(8,128)(2,1)} %get-tuple-element.21, bf16[1024,2048]{1,0:T(8,128)(2,1)} %all-gather.3.cloned.1.call-done, f32[2048]{0:T(1024)S(1)} %bitcast.70, f32[2048]{0:T(1024)S(1)} %bitcast.67, ...), kind=kOutput, calls=%fused_computation.17 | convolution fusion | flops 8615100416 | bytes 25198592 | tf_op jit(solution)/shard_map/dot_general | solution.py:29
  226.6 15.1 %convert_reduce_fusion.1 = (f32[2048]{0:T(1024)S(1)}, bf16[1024,2048]{1,0:T(8,128)(2,1)S(1)}) fusion(f32[1024,2048]{1,0:T(8,128)} %get-tuple-element.56, f32[2048]{0:T(1024)S(1)} %bitcast.66, bf16[1024,2048]{1,0:T(8,128)(2,1)S(1)} %copy-done.3, bf16[2048,2048]{1,0:T(8,128)(2,1)} %get-tuple-element.22), kind=kOutput, calls=%fused_computation.11 | convolution fusion | flops 8617195520 | bytes 25182208 | tf_op jit(solution)/shard_map/dot_general | solution.py:29
  241.8 1.9 copy-done.12
  243.7 13.2 %fusion.20 = f32[1024,2048]{1,0:T(8,128)} fusion(bf16[1024,2048]{1,0:T(8,128)(2,1)S(1)} %get-tuple-element.58, bf16[2048,2048]{1,0:T(8,128)(2,1)} %get-tuple-element.21), kind=kOutput, calls=%fused_computation.60 | convolution fusion | flops 8589934592 | bytes 20971520 | tf_op jit(solution)/shard_map/dot_general | solution.py:423
  256.9 1.3 copy-done.1
  258.3 6.2 convolution_convert_fusion.4.g_ref
  264.5 12.4 %attend_bwd.1 = (bf16[1024,1536]{1,0:T(8,128)(2,1)}, f32[1,1536]{1,0:T(1,128)}) custom-call(s32[1]{0:T(128)} %copy.55.len_ref, bf16[1024,512]{1,0:T(8,128)(2,1)} %get-tuple-element.26.q_ref, bf16[1024,512]{1,0:T(8,128)(2,1)} %get-tuple-element.27.k_ref, bf16[1024,512]{1,0:T(8,128)(2,1)} %get-tuple-element.28.v_ref, ...), custom_call_target="tpu_custom_call" | custom-call | flops 5368709120 | bytes 10485760 | tf_op jit(solution)/shard_map/attend_bwd/pallas_call | solution.py:117
  276.9 17.4 %fusion.15 = (f32[2048]{0:T(1024)S(1)}, f32[2048]{0:T(1024)S(1)}, bf16[1024,2048]{1,0:T(8,128)(2,1)}, f32[2048]{0:T(1024)S(1)}, f32[2048]{0:T(1024)S(1)}, /*index=5*/f32[1024,2048]{1,0:T(8,128)}) fusion(f32[1024]{0:T(1024)S(1)} %add_rsqrt_fusion, f32[1024]{0:T(1024)S(1)} %broadcast_multiply_fusion, bf16[1024,2048]{1,0:T(8,128)(2,1)} %all-gather.3.cloned.1.call-done, ...), kind=kOutput, calls=%fused_computation.55 | convolution fusion | flops 6469705728 | bytes 34660352 | tf_op jit(solution)/shard_map/dot_general | solution.py:29
  294.4 11.9 %convolution_convert_fusion.2 = bf16[2048,1536]{1,0:T(8,128)(2,1)} fusion(bf16[1024,1536]{1,0:T(8,128)(2,1)} %get-tuple-element.29, bf16[1024,2048]{1,0:T(8,128)(2,1)} %all-gather.3.cloned.1.call-done, f32[2048]{0:T(1024)S(1)} %bitcast.80, f32[2048]{0:T(1024)S(1)} %bitcast.78, f32[1024]{0:T(1024)S(1)} %add_rsqrt_fusion, f32[1024]{0:T(1024)S(1)} %broadcast_multiply_fusion), kind=kOutput, calls=%fused_computation.22 | convolution fusion | flops 6458179584 | bytes 13656064 | tf_op jit(solution)/shard_map/dot_general | solution.py:23
  306.3 13.6 %fusion.19 = f32[1024,2048]{1,0:T(8,128)S(1)} fusion(bf16[1024,2048]{1,0:T(8,128)(2,1)} %get-tuple-element.55, bf16[2048,2048]{1,0:T(8,128)(2,1)} %get-tuple-element.22), kind=kOutput, calls=%fused_computation.59 | convolution fusion | flops 8589934592 | bytes 20971520 | tf_op jit(solution)/shard_map/dot_general | solution.py:405
  319.9 4.3 add_convert_fusion.1
  324.2 14.7 %convolution_convert_fusion.1 = bf16[2048,2048]{1,0:T(8,128)(2,1)} fusion(bf16[1024,2048]{1,0:T(8,128)(2,1)} %copy-done.12, bf16[1024,2048]{1,0:T(8,128)(2,1)} %all-gather.3.cloned.1.call-done, f32[2048]{0:T(1024)S(1)} %bitcast.71, f32[2048]{0:T(1024)S(1)} %bitcast.69, f32[1024]{0:T(1024)S(1)} %add_rsqrt_fusion, f32[1024]{0:T(1024)S(1)} %broadcast_multiply_fusion), kind=kOutput, calls=%fused_computation.21 | convolution fusion | flops 8606711808 | bytes 16801792 | tf_op jit(solution)/shard_map/dot_general | solution.py:23
  339.0 14.3 %convolution_convert_fusion = bf16[2048,2048]{1,0:T(8,128)(2,1)} fusion(bf16[1024,2048]{1,0:T(8,128)(2,1)} %get-tuple-element.55, bf16[1024,2048]{1,0:T(8,128)(2,1)} %copy-done.2), kind=kOutput, calls=%fused_computation.20 | convolution fusion | flops 8594128896 | bytes 16777216 | tf_op jit(solution)/shard_map/dot_general | solution.py:23
  353.3 0.6 copy-done.9
  353.9 0.1 dynamic-slice.3
  354.0 0.1 dynamic_update_slice.8
  354.1 0.6 copy.46
  354.7 0.1 dynamic_update_slice.9
  354.8 0.6 copy.47
  355.4 0.6 pad_maximum_fusion.1
  356.0 0.6 pad_maximum_fusion
  356.6 1.8 convert_element_type.151
  358.4 21.1 %reduce-scatter.9.cloned.1.call-done = bf16[256,2048]{1,0:T(8,128)(2,1)} async-done(((bf16[1024,2048]{1,0:T(8,128)(2,1)}), bf16[256,2048]{1,0:T(8,128)(2,1)}) %reduce-scatter.9.cloned.1.call-update) | async-done | bytes 1048592 | tf_op jit(solution)/shard_map/reduce_scatter | solution.py:440
  379.6 2.5 convert_reduce_fusion.2
  382.0 63.1 %reduce-scatter.11.cloned.1.call-done = bf16[256,1536]{1,0:T(8,128)(2,1)} async-done(((bf16[2048,1536]{1,0:T(8,128)(2,1)}), bf16[256,1536]{1,0:T(8,128)(2,1)}) %reduce-scatter.11.cloned.1.call-update) | async-done | bytes 786448 | tf_op jit(solution)/shard_map/reduce_scatter | solution.py:443
  445.1 2.7 reshape.129
  447.8 1.1 copy.41
  448.9 5.1 all-to-all-start
  454.1 4.4 convert_reduce_fusion.3
  458.5 82.5 %reduce-scatter.7.cloned.1.call-done = bf16[256,2048]{1,0:T(8,128)(2,1)} async-done(((bf16[1024,2048]{1,0:T(8,128)(2,1)}), bf16[256,2048]{1,0:T(8,128)(2,1)}) %reduce-scatter.7.cloned.1.call-update) | async-done | bytes 1048592 | tf_op jit(solution)/shard_map/reduce_scatter | solution.py:408
  541.0 2.6 add_convert_fusion.4
  543.6 0.2 convert_bitcast_fusion
  543.8 1.0 copy.42
  544.8 2.2 reshape.136
  547.0 67.4 %reduce-scatter.15.cloned.1.call-done = bf16[256,2048]{1,0:T(8,128)(2,1)} async-done(((bf16[2048,2048]{1,0:T(8,128)(2,1)}), bf16[256,2048]{1,0:T(8,128)(2,1)}) %reduce-scatter.15.cloned.1.call-update) | async-done | bytes 1048592 | tf_op jit(solution)/shard_map/reduce_scatter | solution.py:420
  614.4 2.8 convert_element_type.153
  617.2 72.4 %reduce-scatter.17.cloned.1.call-done = bf16[256,2048]{1,0:T(8,128)(2,1)} async-done(((bf16[2048,2048]{1,0:T(8,128)(2,1)}), bf16[256,2048]{1,0:T(8,128)(2,1)}) %reduce-scatter.17.cloned.1.call-update) | async-done | bytes 1048592 | tf_op jit(solution)/shard_map/reduce_scatter | solution.py:417
  689.6 2.8 convert_element_type.156
  692.3 129.4 %all-reduce.3.cloned.1.call-done = (f32[2,2048]{1,0:T(2,128)}, f32[2,2048]{1,0:T(2,128)}, f32[3,2048]{1,0:T(4,128)}, f32[8192]{0:T(1024)}, f32[2048]{0:T(1024)}) async-done(((f32[2,2048]{1,0:T(2,128)}, f32[2,2048]{1,0:T(2,128)}, f32[3,2048]{1,0:T(4,128)}, f32[8192]{0:T(1024)}, f32[2048]{0:T(1024)}), (f32[2,2048]{1,0:T(2,128)}, f32[2,2048]{1,0:T(2,128)}, f32[3,2048]{1,0:T(4,128)}, f32[8192]{0:T(1024)}, ...) | async-done | bytes 98320 | tf_op jit(solution)/shard_map/psum | solution.py:471
  821.8 1.3 copy.56
  823.1 1.3 copy.57
  824.4 1.4 copy.58
  825.8 1.4 copy.59
  827.2 1.3 copy.60
  (57 shorter events, 0.6 us)
Async XLA Ops:
  7.2 128.7 %copy-start.6 = (bf16[2,2048]{1,0:T(2,128)(2,1)S(1)}, bf16[2,2048]{1,0:T(2,128)(2,1)}, u32[]{:S(2)}) copy-start(bf16[2,2048]{1,0:T(2,128)(2,1)} %param.15) | copy-start | bytes 24580
  7.2 128.8 %copy-start.7 = (bf16[2,2048]{1,0:T(2,128)(2,1)S(1)}, bf16[2,2048]{1,0:T(2,128)(2,1)}, u32[]{:S(2)}) copy-start(bf16[2,2048]{1,0:T(2,128)(2,1)} %param.16) | copy-start | bytes 24580
  7.2 128.8 %all-gather.3.cloned.1.call-start = ((), (), s32[]{:S(2)}) async-start(), calls=%async_computation.8 | async-start | bytes 5242880 | tf_op jit(solution)/shard_map/all_gather | solution.py:367
  7.9 186.1 %all-gather.5.cloned.1.call-start = ((), (), s32[]{:S(2)}) async-start(), calls=%async_computation.10 | async-start | bytes 5242880 | tf_op jit(solution)/shard_map/all_gather | solution.py:368
  136.0 6.4 copy-start
  163.6 35.0 %copy-start.11 = (bf16[1024,512]{1,0:T(8,128)(2,1)S(1)}, bf16[1024,512]{1,0:T(8,128)(2,1)}, u32[]{:S(2)}) copy-start(bf16[1024,512]{1,0:T(8,128)(2,1)} %get-tuple-element.24) | copy-start | bytes 3145732
  196.6 1.9 copy-start.2
  202.4 54.4 %all-to-all-start.1 = ((bf16[2,4,64,2048]{3,2,0,1:T(8,128)(2,1)}), bf16[2,4,64,2048]{3,2,0,1:T(8,128)(2,1)S(1)}, u32[]{:S(2)}, u32[]{:S(2)}) async-start(bf16[2,4,64,2048]{3,2,0,1:T(8,128)(2,1)} %copy.44), calls=%async_computation.4 | async-start | bytes 4194304 | tf_op jit(solution)/shard_map/all_to_all | solution.py:427
  209.2 147.4 %reduce-scatter.13.cloned.1.call-start = ((), (), s32[]{:S(2)}) async-start(), calls=%async_computation.13 | async-start | bytes 2359296 | tf_op jit(solution)/shard_map/reduce_scatter | solution.py:434
  209.2 17.4 %copy-start.3 = (bf16[1024,2048]{1,0:T(8,128)(2,1)S(1)}, bf16[1024,2048]{1,0:T(8,128)(2,1)}, u32[]{:S(2)}) copy-start(bf16[1024,2048]{1,0:T(8,128)(2,1)} %copy-done.2) | copy-start | bytes 12582916
  241.8 1.9 copy-start.12
  256.9 1.3 copy-start.1
  258.2 121.3 %reduce-scatter.9.cloned.1.call-start = ((), (), s32[]{:S(2)}) async-start(), calls=%async_computation.11 | async-start | bytes 5242880 | tf_op jit(solution)/shard_map/reduce_scatter | solution.py:440
  294.3 150.8 %reduce-scatter.11.cloned.1.call-start = ((), (), s32[]{:S(2)}) async-start(), calls=%async_computation.12 | async-start | bytes 7077888 | tf_op jit(solution)/shard_map/reduce_scatter | solution.py:443
  306.2 234.7 %reduce-scatter.7.cloned.1.call-start = ((), (), s32[]{:S(2)}) async-start(), calls=%async_computation.9 | async-start | bytes 5242880 | tf_op jit(solution)/shard_map/reduce_scatter | solution.py:408
  306.3 13.6 %copy-start.10 = (bf16[512,2048]{1,0:T(8,128)(2,1)S(1)}, bf16[512,2048]{1,0:T(8,128)(2,1)}, u32[]{:S(2)}) copy-start(bf16[512,2048]{1,0:T(8,128)(2,1)} %get-tuple-element.25) | copy-start | bytes 6291460
  324.2 290.2 %reduce-scatter.15.cloned.1.call-start = ((), (), s32[]{:S(2)}) async-start(), calls=%async_computation.14 | async-start | bytes 9437184 | tf_op jit(solution)/shard_map/reduce_scatter | solution.py:420
  338.9 350.6 %reduce-scatter.17.cloned.1.call-start = ((), (), s32[]{:S(2)}) async-start(), calls=%async_computation.15 | async-start | bytes 9437184 | tf_op jit(solution)/shard_map/reduce_scatter | solution.py:417
  353.2 0.7 copy-start.9
  353.2 0.8 copy-start.8
  353.3 187.7 %copy-start.4 = (bf16[256,2048]{1,0:T(8,128)(2,1)S(1)}, bf16[256,2048]{1,0:T(8,128)(2,1)}, u32[]{:S(2)}) copy-start(bf16[256,2048]{1,0:T(8,128)(2,1)} %param.12) | copy-start | bytes 3145732
  379.6 74.5 %copy-start.5 = (bf16[256,2048]{1,0:T(8,128)(2,1)S(1)}, bf16[256,2048]{1,0:T(8,128)(2,1)}, u32[]{:S(2)}) copy-start(bf16[256,2048]{1,0:T(8,128)(2,1)} %reduce-scatter.9.cloned.1.call-done) | copy-start | bytes 3145732
  448.9 94.7 %all-to-all-start = ((bf16[4,64,3,1,512]{4,1,3,2,0:T(8,128)(2,1)}), bf16[4,64,3,1,512]{4,1,3,2,0:T(8,128)(2,1)S(1)}, u32[]{:S(2)}, u32[]{:S(2)}) async-start(bf16[4,64,3,1,512]{4,1,3,2,0:T(8,128)(2,1)} %copy.41), calls=%async_computation.3 | async-start | bytes 1572864 | tf_op jit(solution)/shard_map/all_to_all | solution.py:446
  454.0 367.7 %all-reduce.3.cloned.1.call-start = ((), (), s32[]{:S(2)}) async-start(), calls=%async_computation.16 | async-start | bytes 212992 | tf_op jit(solution)/shard_map/psum | solution.py:471
Sparse Core Ops, SparseCore 0:
  9.6 103.3 all-gather.2
  114.6 79.4 all-gather.4
  258.4 42.1 reduce-scatter.12
  302.8 76.7 reduce-scatter.8
  382.8 62.2 reduce-scatter.10
  447.4 93.5 reduce-scatter.6
  544.4 69.8 reduce-scatter.14
  618.2 71.2 reduce-scatter.16
  697.1 124.5 all-reduce.2

commit v3 on v2

--- a/solution.py
+++ b/solution.py
@@ -314,6 +314,347 @@
         name="gather_weights",
     )(qkv_weight, out_weight, up_weight, down_weight)
 
+CHUNK = 512
+
+
+def back_kernel(sp_size, hidden_hbm, cot_hbm, pre_hbm, mlp_hbm, attn_hbm, proj_hbm, ctx_hbm, small_ref,
+                down_out, up_out, qkv_out, dense_out, small_out,
+                left_a, right_a, left_b, right_b, ctx, lent,
+                down_sum, up_sum, qkv_sum, dense_sum, down_sib, up_sib, qkv_sib, dense_sib,
+                down_one, up_one, qkv_one, dense_one, down_two, up_two, qkv_two, dense_two, dense_part,
+                small_acc, small_in, small_z,
+                load_sem, store_sem, sib_send, sib_recv, one_send, one_recv, two_send, two_recv,
+                slab_send, slab_recv, turn_send, turn_recv, small_send, small_recv, z_send, z_recv):
+    dp, sp = lax.axis_index("dp"), lax.axis_index("sp")
+    full, low = jnp.float32, jnp.bfloat16
+    core, chip = dp % 2, dp // 2
+    x, y = chip % 2, chip // 2
+    per = 2
+    pair, lane = dp // per, dp % per
+    turn_dp = sp * per + lane
+    sibling = dp + 1 - 2 * core
+    across_x, across_y = dp + 2 - 4 * x, dp + 4 - 8 * y
+    first = across_y * (1 - core) + across_x * core
+    second = across_x * (1 - core) + across_y * core
+    first_mask, second_mask = 2 - core, 1 + core
+    units = down_sum.shape[1]
+    slab_width = qkv_sum.shape[2]
+    head_width = slab_width // 3
+    rows = dense_one.shape[1]
+    wide = right_a.shape[1]
+
+    def chip_of(mask):
+        return lax.rem(x + lax.rem(mask, 2), 2) + 2 * lax.rem(y + mask // 2, 2)
+
+    def load(source, target, which):
+        return pltpu.make_async_copy(source, target, load_sem.at[which])
+
+    loads = [load(hidden_hbm, left_a, 0), load(cot_hbm, right_a, 1), load(ctx_hbm, ctx, 2),
+             load(pre_hbm, left_b, 3), load(mlp_hbm, right_b, 4)]
+    for c in loads:
+        c.start()
+
+    barrier = pltpu.get_barrier_semaphore()
+    for other in (first, second, sibling):
+        pl.semaphore_signal(barrier, inc=1, device_id=(other, sp), device_id_type=MESH)
+    for step in range(1, sp_size):
+        pl.semaphore_signal(barrier, inc=1, device_id=(dp, lax.rem(sp + step, sp_size)), device_id_type=MESH)
+
+    @pl.when(pair != sp)
+    def _():
+        pl.semaphore_signal(barrier, inc=1, device_id=(turn_dp, pair), device_id_type=MESH)
+
+    pl.semaphore_wait(barrier, 2 + sp_size + jnp.where(pair != sp, 1, 0))
+
+    def remote(source, target, send, recv, device):
+        return pltpu.make_async_remote_copy(
+            src_ref=source, dst_ref=target, send_sem=send, recv_sem=recv,
+            device_id=device, device_id_type=MESH)
+
+    def small_copy(stage):
+        return remote(small_ref if stage == 0 else small_acc.at[stage - 1], small_in.at[stage],
+                      small_send.at[stage], small_recv.at[stage], ((sibling, across_x, across_y)[stage], sp))
+
+    def small_step(stage):
+        small_copy(stage).wait_recv()
+        before = small_ref[...] if stage == 0 else small_acc[stage - 1]
+        small_acc[stage] = before + small_in[stage]
+
+    def z_copy(step):
+        return remote(small_acc.at[2], small_z.at[sp], z_send.at[step - 1], z_recv.at[step - 1],
+                      (dp, lax.rem(sp + step, sp_size)))
+
+    def z_arrival(step):
+        origin = lax.rem(sp + sp_size - step, sp_size)
+        return remote(small_acc.at[2], small_z.at[origin], z_send.at[step - 1], z_recv.at[step - 1], (dp, origin))
+
+    small_copy(0).start()
+
+    class Wide:
+        def __init__(self, index, left, right, width, sums, sib, one, two):
+            self.index, self.left, self.right, self.width = index, left, right, width
+            self.sums, self.sib, self.one, self.two = sums, sib, one, two
+
+        def product(self, block, store):
+            at = pl.ds(pl.multiple_of(block * units, units), units)
+
+            def columns(part, carry):
+                to = pl.ds(pl.multiple_of(part * CHUNK, CHUNK), CHUNK)
+                store(to, lax.dot_general(
+                    self.left[:, at], self.right[:, to], (((0,), (0,)), ((), ())),
+                    preferred_element_type=full))
+                return carry
+            lax.fori_loop(0, self.width // CHUNK, columns, 0)
+
+        def lend(self, slot):
+            return lent.at[slot, :, :self.width]
+
+        def sib_copy(self, slot):
+            place = chip_of(3 - slot)
+            return remote(self.lend(slot), self.sib.at[place], sib_send.at[self.index, slot],
+                          sib_recv.at[self.index, slot], (sibling, sp))
+
+        def for_sibling(self, previous):
+            def step(slot, carry):
+                if previous is not None:
+                    previous.sib_copy(slot).wait_send()
+                block = chip_of(3 - slot) * 2 + 1 - core
+
+                def store(to, total):
+                    lent[slot, :, to] = total.astype(low)
+                self.product(block, store)
+                self.sib_copy(slot).start()
+                return carry
+            lax.fori_loop(0, 4, step, 0)
+
+        def own(self, mask, slot):
+            place = chip_of(mask)
+            self.sib_copy(slot).wait_recv()
+
+            def store(to, total):
+                self.sums[mask, :, to] = (total + self.sib[place, :, to].astype(full)).astype(low)
+            self.product(place * 2 + core, store)
+
+        def first_copy(self, slot):
+            mask = 3 - slot * (1 + core)
+            return remote(self.sums.at[mask], self.one.at[slot], one_send.at[self.index, slot],
+                          one_recv.at[self.index, slot], (first, sp))
+
+        def for_self(self):
+            def leave(slot, carry):
+                mask = 3 - slot * (1 + core)
+                self.own(mask, 3 - mask)
+                self.first_copy(slot).start()
+                return carry
+            lax.fori_loop(0, 2, leave, 0)
+
+            def stay(slot, carry):
+                mask = second_mask * (1 - slot)
+                self.own(mask, 3 - mask)
+                return carry
+            lax.fori_loop(0, 2, stay, 0)
+
+        def second_copy(self):
+            return remote(self.sums.at[second_mask], self.two, two_send.at[self.index],
+                          two_recv.at[self.index], (second, sp))
+
+        def block(self, mask):
+            return self.sums.at[mask]
+
+    class Dense(Wide):
+        def sib_copy(self, slot):
+            return remote(dense_part.at[0], self.sib, sib_send.at[self.index, 0],
+                          sib_recv.at[self.index, 0], (sibling, sp))
+
+        def for_sibling(self, previous):
+            def store(to, total):
+                dense_part[0, :, to] = total.astype(low)
+            self.product(1 - core, store)
+            self.sib_copy(0).start()
+
+        def block(self, mask):
+            return self.sums.at[pl.ds(pl.multiple_of(chip_of(mask) * rows, rows), rows)]
+
+        def first_copy(self, slot):
+            mask = 3 - slot * (1 + core)
+            return remote(self.block(mask), self.one.at[slot], one_send.at[self.index, slot],
+                          one_recv.at[self.index, slot], (first, sp))
+
+        def for_self(self):
+            self.sib_copy(0).wait_recv()
+
+            def store(to, total):
+                self.sums[:, to] = (total + self.sib[:, to].astype(full)).astype(low)
+            self.product(core, store)
+            for slot in (0, 1):
+                self.first_copy(slot).start()
+
+        def second_copy(self):
+            return remote(self.block(second_mask), self.two, two_send.at[self.index],
+                          two_recv.at[self.index], (second, sp))
+
+    down = Wide(0, left_a, right_a, wide, down_sum, down_sib, down_one, down_two)
+    dense = Dense(1, ctx, right_a, wide, dense_sum, dense_sib, dense_one, dense_two)
+    up = Wide(2, left_b, right_b, wide, up_sum, up_sib, up_one, up_two)
+    qkv = Wide(3, left_a, right_a, slab_width, qkv_sum, qkv_sib, qkv_one, qkv_two)
+
+    def add_into(target, *others):
+        height = target.shape[0]
+        step_rows = 32
+
+        def step(i, carry):
+            at = pl.ds(pl.multiple_of(i * step_rows, step_rows), step_rows)
+            total = target[at, :].astype(full)
+            for other in others:
+                total = total + other[at, :].astype(full)
+            target[at, :] = total.astype(low)
+            return carry
+        lax.fori_loop(0, height // step_rows, step, 0)
+
+    def onward(array):
+        array.first_copy(0).wait_recv()
+        add_into(array.block(second_mask), array.one.at[0])
+        array.second_copy().start()
+
+    def finish(array):
+        array.first_copy(1).wait_recv()
+        array.second_copy().wait_recv()
+        add_into(array.block(0), array.one.at[1], array.two)
+
+    loads[0].wait()
+    loads[1].wait()
+    down.for_sibling(None)
+    small_step(0)
+    small_copy(1).start()
+    down.for_self()
+    loads[2].wait()
+    dense.for_sibling(None)
+    small_step(1)
+    small_copy(2).start()
+    dense.for_self()
+    late = [load(attn_hbm, left_a, 0), load(proj_hbm, right_a.at[:, :slab_width], 1)]
+    for c in late:
+        c.start()
+    loads[3].wait()
+    loads[4].wait()
+    up.for_sibling(down)
+    onward(down)
+    small_step(2)
+    for step in range(1, sp_size):
+        z_copy(step).start()
+    small_z[sp] = small_acc[2]
+    up.for_self()
+    for c in late:
+        c.wait()
+    onward(dense)
+    qkv.for_sibling(up)
+    qkv.for_self()
+    onward(up)
+    finish(down)
+    stores = [pltpu.make_async_copy(down.block(0), down_out, store_sem.at[0])]
+    stores[0].start()
+    finish(dense)
+
+    def turn(target):
+        return remote(dense.block(0), target, turn_send, turn_recv, (turn_dp, pair))
+
+    @pl.when(pair != sp)
+    def _():
+        turn(dense_out).start()
+
+    @pl.when(pair == sp)
+    def _():
+        c = pltpu.make_async_copy(dense.block(0), dense_out, store_sem.at[1])
+        c.start()
+        c.wait()
+
+    onward(qkv)
+    finish(up)
+    stores.append(pltpu.make_async_copy(up.block(0), up_out, store_sem.at[2]))
+    stores[1].start()
+    for step in range(1, sp_size):
+        z_arrival(step).wait_recv()
+    total = small_z[0]
+    for place in range(1, sp_size):
+        total = total + small_z[place]
+    small_out[...] = total
+    finish(qkv)
+
+    def slab_rows(owner):
+        return pl.ds(pl.multiple_of(owner * rows, rows), rows)
+
+    def slab_copy(step, part, origin, there):
+        at = pl.ds(pl.multiple_of(part * wide + origin * head_width, head_width), head_width)
+        return remote(qkv_sum.at[0, slab_rows(there), pl.ds(part * head_width, head_width)], qkv_out.at[:, at],
+                      slab_send.at[step - 1, part], slab_recv.at[step - 1, part], (dp, there))
+
+    for step in range(1, sp_size):
+        for part in range(3):
+            slab_copy(step, part, sp, lax.rem(sp + step, sp_size)).start()
+    for part in range(3):
+        at = pl.ds(pl.multiple_of(part * wide + sp * head_width, head_width), head_width)
+        c = pltpu.make_async_copy(qkv_sum.at[0, slab_rows(sp), pl.ds(part * head_width, head_width)],
+                                  qkv_out.at[:, at], store_sem.at[3 + part])
+        c.start()
+        stores.append(c)
+    for step in range(1, sp_size):
+        for part in range(3):
+            slab_copy(step, part, lax.rem(sp + sp_size - step, sp_size), sp).wait_recv()
+
+    @pl.when(pair != sp)
+    def _():
+        turn(dense_out).wait_recv()
+        turn(dense_out).wait_send()
+
+    for c in stores:
+        c.wait()
+    for slot in range(4):
+        qkv.sib_copy(slot).wait_send()
+    dense.sib_copy(0).wait_send()
+    for array in (down, dense, up, qkv):
+        for slot in (0, 1):
+            array.first_copy(slot).wait_send()
+        array.second_copy().wait_send()
+    for stage in range(3):
+        small_copy(stage).wait_send()
+    for step in range(1, sp_size):
+        z_copy(step).wait_send()
+        for part in range(3):
+            slab_copy(step, part, sp, lax.rem(sp + step, sp_size)).wait_send()
+
+def reduce_gradients(sp_size, rows, hidden, grad_out, grad_pre, mlp_in, attn_in, grad_proj, context, small):
+    seq, wide = mlp_in.shape
+    slab_width = grad_proj.shape[1]
+    units = 4 * rows
+    full, low = jnp.float32, jnp.bfloat16
+    hbm = pl.BlockSpec(memory_space=pltpu.HBM)
+    vmem = pl.BlockSpec(memory_space=pltpu.VMEM)
+    dma = pltpu.SemaphoreType.DMA
+    def v(*shape, kind=low):
+        return pltpu.VMEM(shape, kind)
+    scratch = [
+        v(seq, wide), v(seq, wide), v(seq, wide), v(seq, wide), v(seq, context.shape[1]), v(4, units, wide),
+        v(4, units, wide), v(4, units, wide), v(4, units, slab_width), v(4 * rows, wide),
+        v(4, units, wide), v(4, units, wide), v(4, units, slab_width), v(4 * rows, wide),
+        v(2, units, wide), v(2, units, wide), v(2, units, slab_width), v(2, rows, wide),
+        v(units, wide), v(units, wide), v(units, slab_width), v(rows, wide),
+        v(1, 4 * rows, wide),
+        v(3, *small.shape, kind=full), v(3, *small.shape, kind=full), v(sp_size, *small.shape, kind=full),
+        dma((5,)), dma((6,)), dma((4, 4)), dma((4, 4)), dma((4, 2)), dma((4, 2)), dma((4,)), dma((4,)),
+        dma((sp_size - 1, 3)), dma((sp_size - 1, 3)), dma, dma, dma((3,)), dma((3,)), dma((sp_size - 1,)), dma((sp_size - 1,)),
+    ]
+    return pl.pallas_call(
+        functools.partial(back_kernel, sp_size),
+        out_shape=[jax.ShapeDtypeStruct((units, wide), low), jax.ShapeDtypeStruct((units, wide), low),
+                   jax.ShapeDtypeStruct((rows, 3 * wide), low), jax.ShapeDtypeStruct((rows, wide), low),
+                   jax.ShapeDtypeStruct(small.shape, full)],
+        in_specs=[hbm] * 7 + [vmem], out_specs=[hbm] * 4 + [vmem],
+        scratch_shapes=scratch,
+        compiler_params=pltpu.CompilerParams(collective_id=1, has_side_effects=True, vmem_limit_bytes=67043328),
+        cost_estimate=pl.CostEstimate(flops=26 * 10 ** 9, bytes_accessed=300 * 1000 * 1000, transcendentals=0),
+        name="reduce_gradients",
+    )(hidden, grad_out, grad_pre, mlp_in, attn_in, grad_proj, context, small)
+
 def gather_plain(dp_size, sp_size, qkv_weight, out_weight, up_weight, down_weight):
     head_width = D // sp_size
     qkv_rows = qkv_weight.shape[0]
@@ -338,6 +679,34 @@
         tiled=True,
     ).reshape(head_width, D)
     return qkv_own, out_own, up_own, down_own
+
+
+def reduce_plain(
+    dp_size, sp_size, rows, hidden, grad_out, grad_pre, mlp_in, attn_in, grad_proj, context
+):
+    def scatter(left, right):
+        return lax.psum_scatter(
+            contract_rows(left, right).astype(jnp.bfloat16), "dp", scatter_dimension=0, tiled=True
+        )
+
+    grad_dense = lax.all_to_all(
+        contract_rows(context, grad_out)
+        .astype(jnp.bfloat16)
+        .reshape(dp_size // sp_size, sp_size, rows, D),
+        "sp",
+        split_axis=1,
+        concat_axis=0,
+        tiled=True,
+    ).reshape(dp_size * rows, D)
+    grad_dense = lax.psum_scatter(grad_dense, "dp", scatter_dimension=0, tiled=True)
+    grad_qkv = lax.all_to_all(
+        scatter(attn_in, grad_proj).reshape(sp_size, rows, 3, 1, D // sp_size),
+        "sp",
+        split_axis=0,
+        concat_axis=3,
+        tiled=True,
+    ).reshape(rows, 3 * D)
+    return scatter(hidden, grad_out), scatter(grad_pre, mlp_in), grad_qkv, grad_dense
 
 
 def body(
@@ -393,7 +762,6 @@
     attn_in = (normed * gains[0] + shifts[0]).astype(low)
     mlp_in = (normed * gains[1] + shifts[1]).astype(low)
     row_valid = positions < length
-    grad_out = jnp.where(row_valid[:, None], seq_cotangent, jnp.zeros_like(seq_cotangent))
 
     projected = jnp.dot(attn_in, qkv_own, preferred_element_type=full)
     queries, key_rows, values, context = attend_fwd(
@@ -412,26 +780,13 @@
         tokens.astype(full) + reduced_out.astype(full) + out_bias.astype(full)
     ).astype(low)
 
+    seq_cotangent, _ = lax.optimization_barrier((seq_cotangent, partial_out))
+    grad_out = jnp.where(row_valid[:, None], seq_cotangent, jnp.zeros_like(seq_cotangent))
     grad_hidden = contract_cols(grad_out, down_own)
     grad_pre = (grad_hidden * gelu_slope(pre_act)).astype(low)
-    grad_down = lax.psum_scatter(
-        contract_rows(hidden, grad_out).astype(low), "dp", scatter_dimension=0, tiled=True
-    )
-    grad_up = lax.psum_scatter(
-        contract_rows(grad_pre, mlp_in).astype(low), "dp", scatter_dimension=0, tiled=True
-    )
     grad_mlp_in = jnp.dot(grad_pre, up_own, preferred_element_type=full)
 
     grad_context = contract_cols(grad_out, out_own).astype(low)
-    grad_dense = contract_rows(context, grad_out).astype(low)
-    grad_dense = lax.all_to_all(
-        grad_dense.reshape(per_shard, sp_size, qkv_rows, D),
-        "sp",
-        split_axis=1,
-        concat_axis=0,
-        tiled=True,
-    ).reshape(dp_size * qkv_rows, D)
-    grad_dense = lax.psum_scatter(grad_dense, "dp", scatter_dimension=0, tiled=True)
     grad_proj, grad_proj_sum = attend_bwd(
         queries, key_rows, values, grad_context, cos_rows, sin_rows, lengths
     )
@@ -440,17 +795,6 @@
     reduced_hat = lax.psum_scatter(
         grad_hat.astype(low), "sp", scatter_dimension=0, tiled=True
     ).astype(full)
-    grad_qkv = lax.psum_scatter(
-        contract_rows(attn_in, grad_proj).astype(low), "dp", scatter_dimension=0, tiled=True
-    )
-    grad_qkv = lax.all_to_all(
-        grad_qkv.reshape(sp_size, qkv_rows, 3, 1, head_width),
-        "sp",
-        split_axis=0,
-        concat_axis=3,
-        tiled=True,
-    ).reshape(qkv_rows, 3 * D)
-
     own_cotangent = lax.dynamic_slice_in_dim(grad_out, shard * own_rows, own_rows, 0).astype(full)
     spread_units = lax.dynamic_update_index_in_dim(
         jnp.zeros((dp_size, sp_size, units), full),
@@ -468,10 +812,48 @@
         [jnp.sum(grad_attn_in * normed, axis=0), jnp.sum(grad_mlp_in * normed, axis=0)]
     )
     shift_grad = jnp.stack([jnp.sum(grad_attn_in, axis=0), jnp.sum(grad_mlp_in, axis=0)])
-    gain_total, shift_total, qkv_bias_total, unit_total, out_bias_total = lax.psum(
-        (gain_grad, shift_grad, spread_bias, spread_units, jnp.sum(own_cotangent, axis=0)),
-        ("dp", "sp"),
-    )
+    out_bias_part = jnp.sum(own_cotangent, axis=0)
+    if square:
+        small = jnp.concatenate(
+            [
+                piece.reshape(-1, 128)
+                for piece in (gain_grad, shift_grad, spread_bias, spread_units, out_bias_part)
+            ]
+        )
+        grad_down, grad_up, grad_qkv, grad_dense, small = reduce_gradients(
+            sp_size,
+            qkv_rows,
+            hidden,
+            grad_out,
+            grad_pre,
+            mlp_in,
+            attn_in,
+            grad_proj,
+            context,
+            small,
+        )
+        small = small.reshape(-1)
+        ends = [2 * D, 4 * D, 7 * D, 7 * D + dp_size * sp_size * units]
+        gain_total, shift_total, qkv_bias_total, unit_total, out_bias_total = jnp.split(small, ends)
+        gain_total = gain_total.reshape(2, D)
+        shift_total = shift_total.reshape(2, D)
+        qkv_bias_total = qkv_bias_total.reshape(3, D)
+    else:
+        grad_down, grad_up, grad_qkv, grad_dense = reduce_plain(
+            dp_size,
+            sp_size,
+            qkv_rows,
+            hidden,
+            grad_out,
+            grad_pre,
+            mlp_in,
+            attn_in,
+            grad_proj,
+            context,
+        )
+        gain_total, shift_total, qkv_bias_total, unit_total, out_bias_total = lax.psum(
+            (gain_grad, shift_grad, spread_bias, spread_units, out_bias_part), ("dp", "sp")
+        )
 
     own_inverse = lax.dynamic_slice_in_dim(inverse, shard * own_rows, own_rows, 0)
     own_normed = lax.dynamic_slice_in_dim(normed, shard * own_rows, own_rows, 0)

time: 841 us -> 523 us (0.62)
  waiting for transfers between devices: 468 us -> 74.3 us
  Pallas kernels: 143 us -> 288 us
  matrix products: 142 us -> 94.6 us
  local copies, waits for them, and re-layouts: 24 us -> 9.64 us
  starting transfers between devices: 12.2 us -> 0.16 us
    reduce_scatter x4 -> x0, waiting for transfers between devices: 203 us -> none  [the longest x1 72.4 us: body(): lax.psum_scatter(contract_rows(hidden, grad_out).astype(low), 'dp', scatt...]
    pallas_call x0 -> x1, Pallas kernels: none -> 145 us  [reduce_gradients(): pl.pallas_call(functools.partial(back_kernel, sp_size), out_shape=[jax.Sh...]
    psum x1 -> x0, waiting for transfers between devices: 129 us -> none  [body(): lax.psum((gain_grad, shift_grad, spread_bias, spread_units, jnp.sum(own_c...]
    reduce_scatter x1, waiting for transfers between devices: 82.5 us -> 0.01 us  [body(): lax.psum_scatter(partial_out.astype(low), 'sp', scatter_dimension=0, tile...]
    reduce_scatter x1, waiting for transfers between devices: 21.1 us -> 72.4 us  [body(): lax.psum_scatter(grad_hat.astype(low), 'sp', scatter_dimension=0, tiled=T...]
    dot_general x4 -> x0, matrix products: 43.3 us -> none  [contract_rows(): lax.dot_general(left, right, (((0,), (0,)), ((), ())), preferred_element_...]
    all_gather x1, waiting for transfers between devices: 30.5 us -> 0.01 us  [body(): seq_cotangent = lax.all_gather(cotangent, 'sp', axis=0, tiled=True)]
    all_to_all x2 -> x0, starting transfers between devices: 11.9 us -> none  [the longest x1 6.76 us: body(): lax.all_to_all(grad_dense.reshape(per_shard, sp_size, qkv_rows, D), 'sp',...]
  transfers between devices with their start and end apart: 11 -> 4, of which waited for: 7 -> 1; matrix products, arithmetic and copies ran while one was open for 21% -> 16% of each run, Pallas kernels for 17% -> 53%
where the time goes in v3:
time: 523 us; the launch traced here: 518 us
  Pallas kernels  288 us (55%)
  matrix products  94.6 us (18%)
  waiting for transfers between devices  74.3 us (14%)
  other arithmetic  36 us (7%)
  between operations  14.9 us (3%)
  local copies, waits for them, and re-layouts  9.64 us (2%)
    pallas_call x1, Pallas kernels, reduce_gradients(): pl.pallas_call(functools.partial(back_kernel, sp_size), out_shape=[jax.Sh...  145 us
    pallas_call x1, Pallas kernels, gather_weights(): pl.pallas_call(functools.partial(gather_kernel, sp_size), out_shape=[jax....  121 us
    reduce_scatter x1, waiting for transfers between devices, body(): lax.psum_scatter(grad_hat.astype(low), 'sp', scatter_dimension=0, tiled=T...  72.4 us
    dot_general x4, matrix products, contract_cols(): lax.dot_general(left, right, (((1,), (1,)), ((), ())), preferred_element_...  55.7 us
    dot_general x1, matrix products, body(): jnp.dot(hidden, down_own, preferred_element_type=full)  13.1 us
    dot_general x1, matrix products, body(): grad_mlp_in = jnp.dot(grad_pre, up_own, preferred_element_type=full)  12.8 us
    pallas_call x1, Pallas kernels, attend_bwd(): pl.pallas_call(functools.partial(bwd_kernel, HEAD ** (-0.5), heads), grid...  12.6 us
  transfers between devices with their start and end apart: 4, of which 1 were waited for; matrix products, arithmetic and copies ran while one was open for 16% of the time, Pallas kernels for 53%

profile of v3, /device:TPU:8, one launch (start us, length us, event | category | flops | bytes accessed | tf_op | source)
XLA Modules:
  0.0 517.6 jit_solution(13523379440340654346)
XLA Ops:
  7.2 0.0 all-gather.3.cloned.1.call-start
  7.2 0.7 all-gather.3.cloned.1.call-update
  7.9 0.0 all-gather.5.cloned.1.call-start
  8.0 0.7 all-gather.5.cloned.1.call-update
  8.7 0.0 reduce-scatter.5.cloned.1.call-start
  8.7 0.8 fusion.16
  9.5 0.8 fusion.17
  10.3 0.7 convert_bitcast_fusion
  11.0 0.6 copy.30
  11.6 0.1 pad.6.clone
  11.7 0.1 pad.9.clone
  12.4 0.7 reshape.132
  13.2 1.9 fusion.12
  15.1 121.1 %gather_weights.1 = (bf16[2048,1536]{1,0:T(8,128)(2,1)}, bf16[512,2048]{1,0:T(8,128)(2,1)}, bf16[2048,2048]{1,0:T(8,128)(2,1)}, bf16[2048,2048]{1,0:T(8,128)(2,1)}) custom-call(bf16[64,6144]{1,0:T(8,128)(2,1)} %qkv_ref.1, bf16[64,2048]{1,0:T(8,128)(2,1)} %out_ref.1, bf16[256,2048]{1,0:T(8,128)(2,1)} %up_ref.1, bf16[256,2048]{1,0:T(8,128)(2,1)} %down_ref.1), custom_call_target="tpu_custom_call" | custom-call | bytes 300000000 | tf_op jit(solution)/shard_map/gather_weights/pallas_call | solution.py:304
  136.2 1.3 maximum_maximum_fusion
  137.6 3.0 convert_reduce_fusion
  140.5 0.0 slice-start.2
  140.5 3.6 fusion.2
  144.2 0.0 slice-start.3
  144.2 4.4 add_convert_fusion.1
  148.7 8.6 %fusion.19.pq.pk.pv = f32[1024,1536]{1,0:T(8,128)} fusion(bf16[1024,2048]{1,0:T(8,128)(2,1)S(1)} %get-tuple-element.53.attn_hbm, bf16[2048,1536]{1,0:T(8,128)(2,1)S(1)} %bitcast.61), kind=kOutput, calls=%fused_computation.61 | convolution fusion | flops 6442450944 | bytes 16777216 | tf_op jit(solution)/shard_map/dot_general | solution.py:766
  157.3 9.3 %attend_fwd.1 = (bf16[1024,512]{1,0:T(8,128)(2,1)}, bf16[1024,512]{1,0:T(8,128)(2,1)}, bf16[1024,512]{1,0:T(8,128)(2,1)}, bf16[1024,512]{1,0:T(8,128)(2,1)}) custom-call(s32[1]{0:T(128)} %copy.37.len_ref, f32[1024,1536]{1,0:T(8,128)} %fusion.19.pq.pk.pv, f32[1024,1536]{1,0:T(8,128)} %fusion.19.pq.pk.pv, f32[1024,1536]{1,0:T(8,128)} %fusion.19.pq.pk.pv, ...), custom_call_target="tpu_custom_call" | custom-call | flops 2147483648 | bytes 12582912 | tf_op jit(solution)/shard_map/attend_fwd/pallas_call | solution.py:79
  166.5 15.1 %multiply_convert_fusion = (bf16[1024,2048]{1,0:T(8,128)(2,1)S(1)}, f32[1024,2048]{1,0:T(8,128)}) fusion(f32[2048]{0:T(1024)S(1)} %bitcast.50, bf16[1024,2048]{1,0:T(8,128)(2,1)} %get-tuple-element.54.mlp_hbm, bf16[2048,2048]{1,0:T(8,128)(2,1)} %get-tuple-element.27), kind=kOutput, calls=%fused_computation.16 | convolution fusion | flops 8602517504 | bytes 25174016 | tf_op jit(solution)/shard_map/dot_general | solution.py:29
  181.7 13.1 %fusion.18 = f32[1024,2048]{1,0:T(8,128)S(1)} fusion(bf16[1024,2048]{1,0:T(8,128)(2,1)S(1)} %get-tuple-element.66.hidden_hbm, bf16[2048,2048]{1,0:T(8,128)(2,1)} %get-tuple-element.28), kind=kOutput, calls=%fused_computation.60 | convolution fusion | flops 8589934592 | bytes 20971520 | tf_op jit(solution)/shard_map/dot_general | solution.py:773
  194.8 4.4 convolution_add_fusion
  199.2 2.5 broadcast_select_fusion.cot_hbm
  201.8 0.0 slice-start
  201.8 6.5 %convolution_convert_fusion.g_ref = bf16[1024,512]{1,0:T(8,128)(2,1)} fusion(bf16[1024,2048]{1,0:T(8,128)(2,1)S(1)} %broadcast_select_fusion.cot_hbm, bf16[512,2048]{1,0:T(8,128)(2,1)} %get-tuple-element.31), kind=kOutput, calls=%fused_computation.31 | convolution fusion | flops 2148007936 | bytes 7340032 | tf_op jit(solution)/shard_map/dot_general | solution.py:29
  208.3 17.1 %convert_reduce_fusion.1 = (f32[2048]{0:T(1024)S(1)}, bf16[1024,2048]{1,0:T(8,128)(2,1)}) fusion(f32[1024,2048]{1,0:T(8,128)} %get-tuple-element.67, f32[2048]{0:T(1024)S(1)} %bitcast.51, bf16[1024,2048]{1,0:T(8,128)(2,1)S(1)} %broadcast_select_fusion.cot_hbm, bf16[2048,2048]{1,0:T(8,128)(2,1)} %get-tuple-element.28), kind=kOutput, calls=%fused_computation.11 | convolution fusion | flops 8617195520 | bytes 25182208 | tf_op jit(solution)/shard_map/dot_general | solution.py:29
  225.4 0.0 slice-done
  225.4 12.8 %fusion.20 = f32[1024,2048]{1,0:T(8,128)} fusion(bf16[1024,2048]{1,0:T(8,128)(2,1)} %get-tuple-element.69.pre_hbm, bf16[2048,2048]{1,0:T(8,128)(2,1)S(1)} %bitcast.59), kind=kOutput, calls=%fused_computation.62 | convolution fusion | flops 8589934592 | bytes 20971520 | tf_op jit(solution)/shard_map/dot_general | solution.py:787
  238.1 12.6 %attend_bwd.1 = (bf16[1024,1536]{1,0:T(8,128)(2,1)}, f32[1,1536]{1,0:T(1,128)}) custom-call(s32[1]{0:T(128)} %copy.37.len_ref, bf16[1024,512]{1,0:T(8,128)(2,1)} %get-tuple-element.33.q_ref, bf16[1024,512]{1,0:T(8,128)(2,1)} %get-tuple-element.34.k_ref, bf16[1024,512]{1,0:T(8,128)(2,1)} %get-tuple-element.35.v_ref, ...), custom_call_target="tpu_custom_call" | custom-call | flops 5368709120 | bytes 10485760 | tf_op jit(solution)/shard_map/attend_bwd/pallas_call | solution.py:117
  250.7 17.1 %fusion.13 = (f32[2048]{0:T(1024)S(1)}, f32[2048]{0:T(1024)S(1)}, bf16[1024,2048]{1,0:T(8,128)(2,1)}, f32[2048]{0:T(1024)S(1)}, f32[2048]{0:T(1024)S(1)}, /*index=5*/f32[1024,2048]{1,0:T(8,128)}) fusion(f32[1024]{0:T(1024)S(1)} %add_rsqrt_fusion, f32[1024]{0:T(1024)S(1)} %broadcast_multiply_fusion, bf16[1024,2048]{1,0:T(8,128)(2,1)} %all-gather.3.cloned.1.call-done, ...), kind=kOutput, calls=%fused_computation.55 | convolution fusion | flops 6469705728 | bytes 34660352 | tf_op jit(solution)/shard_map/dot_general | solution.py:29
  267.8 0.0 reduce-scatter.5.cloned.1.call-update
  267.8 0.0 reduce-scatter.3.cloned.1.call-start
  267.9 0.5 reduce-scatter.3.cloned.1.call-update
  268.4 0.1 copy-done.8
  268.5 0.6 convert_element_type.116
  269.2 0.1 dynamic_update_slice.8
  269.3 0.1 dynamic_update_slice.9
  269.4 0.1 dynamic-slice.3
  269.5 0.6 constant_dynamic-update-slice_fusion.4
  270.1 0.6 constant_dynamic-update-slice_fusion.3
  270.7 0.6 constant_dynamic-update-slice_fusion.2
  271.3 0.6 constant_dynamic-update-slice_fusion.1
  271.9 72.4 %reduce-scatter.5.cloned.1.call-done = bf16[256,2048]{1,0:T(8,128)(2,1)} async-done(((bf16[1024,2048]{1,0:T(8,128)(2,1)}), bf16[256,2048]{1,0:T(8,128)(2,1)}) %reduce-scatter.5.cloned.1.call-update) | async-done | bytes 1048592 | tf_op jit(solution)/shard_map/reduce_scatter | solution.py:795
  344.3 2.4 convert_reduce_fusion.2
  346.7 4.0 convert_reduce_fusion.3
  350.7 0.6 constant_dynamic-update-slice_fusion.small_ref
  351.3 144.9 %reduce_gradients.1 = (bf16[256,2048]{1,0:T(8,128)(2,1)}, bf16[256,2048]{1,0:T(8,128)(2,1)}, bf16[64,6144]{1,0:T(8,128)(2,1)}, bf16[64,2048]{1,0:T(8,128)(2,1)}, f32[192,128]{1,0:T(8,128)}) custom-call(bf16[1024,2048]{1,0:T(8,128)(2,1)} %copy-done.11, bf16[1024,2048]{1,0:T(8,128)(2,1)} %copy-done.1, bf16[1024,2048]{1,0:T(8,128)(2,1)} %get-tuple-element.69.pre_hbm, ...), custom_call_target="tpu_custom_call" | custom-call | flops 25999998976 | bytes 300000000 | tf_op jit(solution)/shard_map/reduce_gradients/pallas_call | solution.py:646
  496.3 0.0 copy-start.4
  496.3 0.0 copy-start.5
  496.3 0.0 copy-start.2
  496.3 0.0 copy-start.6
  496.3 2.9 convert_element_type.127
  499.2 2.8 convert_element_type.128
  502.0 2.4 convert_element_type.125
  504.4 0.8 convert_element_type.126
  505.2 0.6 reshape.139
  505.8 0.6 reshape.137
  506.5 0.6 reshape.138
  507.1 0.6 slice_bitcast_fusion.1
  507.7 0.6 slice_bitcast_fusion
  508.3 2.6 add_convert_fusion.3
  (48 shorter events, 0.2 us)
Async XLA Ops:
  7.2 130.4 %all-gather.3.cloned.1.call-start = ((), (), s32[]{:S(2)}) async-start(), calls=%async_computation.2 | async-start | bytes 5242880 | tf_op jit(solution)/shard_map/all_gather | solution.py:736
  7.9 191.3 %all-gather.5.cloned.1.call-start = ((), (), s32[]{:S(2)}) async-start(), calls=%async_computation.4 | async-start | bytes 5242880 | tf_op jit(solution)/shard_map/all_gather | solution.py:737
  8.7 335.7 %reduce-scatter.5.cloned.1.call-start = ((), (), s32[]{:S(2)}) async-start(), calls=%async_computation.5 | async-start | bytes 5242880 | tf_op jit(solution)/shard_map/reduce_scatter | solution.py:795
  137.6 6.6 %copy-start = (bf16[1024,2048]{1,0:T(8,128)(2,1)S(1)}, bf16[1024,2048]{1,0:T(8,128)(2,1)}, u32[]{:S(2)}) copy-start(bf16[1024,2048]{1,0:T(8,128)(2,1)} %all-gather.3.cloned.1.call-done) | copy-start | bytes 12582916
  140.5 8.1 %slice-start.2 = ((s8[6291456]{0:T(1024)(128)(4,1)}), s8[4194304]{0:T(1024)(128)(4,1)S(1)}, s32[]{:S(2)}) async-start(s8[6291456]{0:T(1024)(128)(4,1)} %bitcast.60), calls=%async_computation.8 | async-start | bytes 8388608
  144.2 4.5 slice-start.3
  148.6 8.6 %copy-start.3 = (bf16[1024,2048]{1,0:T(8,128)(2,1)}, bf16[1024,2048]{1,0:T(8,128)(2,1)S(1)}, u32[]{:S(2)}) copy-start(bf16[1024,2048]{1,0:T(8,128)(2,1)S(1)} %get-tuple-element.53.attn_hbm) | copy-start | bytes 12582916
  181.6 13.1 %copy-start.11 = (bf16[1024,2048]{1,0:T(8,128)(2,1)}, bf16[1024,2048]{1,0:T(8,128)(2,1)S(1)}, u32[]{:S(2)}) copy-start(bf16[1024,2048]{1,0:T(8,128)(2,1)S(1)} %get-tuple-element.66.hidden_hbm) | copy-start | bytes 12582916
  181.7 13.1 %copy-start.9 = (bf16[512,2048]{1,0:T(8,128)(2,1)S(1)}, bf16[512,2048]{1,0:T(8,128)(2,1)}, u32[]{:S(2)}) copy-start(bf16[512,2048]{1,0:T(8,128)(2,1)} %get-tuple-element.31) | copy-start | bytes 6291460
  181.7 13.1 %copy-start.10 = (bf16[1024,512]{1,0:T(8,128)(2,1)S(1)}, bf16[1024,512]{1,0:T(8,128)(2,1)}, u32[]{:S(2)}) copy-start(bf16[1024,512]{1,0:T(8,128)(2,1)} %get-tuple-element.30.ctx_hbm) | copy-start | bytes 3145732
  201.8 23.6 %copy-start.1 = (bf16[1024,2048]{1,0:T(8,128)(2,1)}, bf16[1024,2048]{1,0:T(8,128)(2,1)S(1)}, u32[]{:S(2)}) copy-start(bf16[1024,2048]{1,0:T(8,128)(2,1)S(1)} %broadcast_select_fusion.cot_hbm) | copy-start | bytes 12582916
  201.8 23.6 %slice-start = ((s8[8388608]{0:T(1024)(128)(4,1)}), s8[4194304]{0:T(1024)(128)(4,1)S(1)}, s32[]{:S(2)}) async-start(s8[8388608]{0:T(1024)(128)(4,1)} %bitcast.58), calls=%async_computation.6 | async-start | bytes 8388608
  208.3 17.1 %slice-start.1 = ((s8[8388608]{0:T(1024)(128)(4,1)}), s8[4194304]{0:T(1024)(128)(4,1)S(1)}, s32[]{:S(2)}) async-start(s8[8388608]{0:T(1024)(128)(4,1)} %bitcast.58), calls=%async_computation.7 | async-start | bytes 8388608
  267.8 0.7 copy-start.8
  267.8 1.4 copy-start.7
  267.8 240.5 %reduce-scatter.3.cloned.1.call-start = ((), (), s32[]{:S(2)}) async-start(), calls=%async_computation.3 | async-start | bytes 5242880 | tf_op jit(solution)/shard_map/reduce_scatter | solution.py:776
  496.3 8.1 %copy-start.4 = (bf16[64,2048]{1,0:T(8,128)(2,1)S(1)}, bf16[64,2048]{1,0:T(8,128)(2,1)}, u32[]{:S(2)}) copy-start(bf16[64,2048]{1,0:T(8,128)(2,1)} %get-tuple-element.40) | copy-start | bytes 786436
  496.3 8.9 %copy-start.5 = (f32[192,128]{1,0:T(8,128)S(1)}, f32[192,128]{1,0:T(8,128)}, u32[]{:S(2)}) copy-start(f32[192,128]{1,0:T(8,128)} %get-tuple-element.38) | copy-start | bytes 294916
  496.3 12.0 %copy-start.2 = (bf16[256,2048]{1,0:T(8,128)(2,1)S(1)}, bf16[256,2048]{1,0:T(8,128)(2,1)}, u32[]{:S(2)}) copy-start(bf16[256,2048]{1,0:T(8,128)(2,1)} %param.12) | copy-start | bytes 3145732
  496.3 12.0 %copy-start.6 = (f32[2048]{0:T(1024)S(1)}, f32[2048]{0:T(1024)}, u32[]{:S(2)}) copy-start(f32[2048]{0:T(1024)} %convert_element_type.116) | copy-start | bytes 24580
Sparse Core Ops, SparseCore 0:
  9.6 106.9 all-gather.2
  118.2 79.3 all-gather.4
  268.0 76.3 reduce-scatter.4
  346.6 94.6 reduce-scatter.2

commit v4 on v3

--- a/solution.py
+++ b/solution.py
@@ -776,10 +776,6 @@
     reduced_out = lax.psum_scatter(
         partial_out.astype(low), "sp", scatter_dimension=0, tiled=True
     )
-    output = (
-        tokens.astype(full) + reduced_out.astype(full) + out_bias.astype(full)
-    ).astype(low)
-
     seq_cotangent, _ = lax.optimization_barrier((seq_cotangent, partial_out))
     grad_out = jnp.where(row_valid[:, None], seq_cotangent, jnp.zeros_like(seq_cotangent))
     grad_hidden = contract_cols(grad_out, down_own)
@@ -794,7 +790,7 @@
     grad_hat = grad_attn_in * gains[0] + grad_mlp_in * gains[1]
     reduced_hat = lax.psum_scatter(
         grad_hat.astype(low), "sp", scatter_dimension=0, tiled=True
-    ).astype(full)
+    )
     own_cotangent = lax.dynamic_slice_in_dim(grad_out, shard * own_rows, own_rows, 0).astype(full)
     spread_units = lax.dynamic_update_index_in_dim(
         jnp.zeros((dp_size, sp_size, units), full),
@@ -820,6 +816,7 @@
                 for piece in (gain_grad, shift_grad, spread_bias, spread_units, out_bias_part)
             ]
         )
+        small, reduced_out = lax.optimization_barrier((small, reduced_out))
         grad_down, grad_up, grad_qkv, grad_dense, small = reduce_gradients(
             sp_size,
             qkv_rows,
@@ -832,6 +829,7 @@
             context,
             small,
         )
+        reduced_hat, small = lax.optimization_barrier((reduced_hat, small))
         small = small.reshape(-1)
         ends = [2 * D, 4 * D, 7 * D, 7 * D + dp_size * sp_size * units]
         gain_total, shift_total, qkv_bias_total, unit_total, out_bias_total = jnp.split(small, ends)
@@ -855,6 +853,11 @@
             (gain_grad, shift_grad, spread_bias, spread_units, out_bias_part), ("dp", "sp")
         )
 
+    output = (
+        tokens.astype(full) + reduced_out.astype(full) + out_bias.astype(full)
+    ).astype(low)
+
+    reduced_hat = reduced_hat.astype(full)
     own_inverse = lax.dynamic_slice_in_dim(inverse, shard * own_rows, own_rows, 0)
     own_normed = lax.dynamic_slice_in_dim(normed, shard * own_rows, own_rows, 0)
     grad_input = own_inverse * (

time: 523 us -> 457 us (0.87)
  waiting for transfers between devices: 74.3 us -> 4.29 us
  local copies, waits for them, and re-layouts: 9.64 us -> 15.2 us
    reduce_scatter x1, waiting for transfers between devices: 72.4 us -> 0.02 us  [body(): lax.psum_scatter(grad_hat.astype(low), 'sp', scatter_dimension=0, tiled=T...]
  transfers between devices with their start and end apart: 4 -> 4, of which waited for: 1 -> 1; matrix products, arithmetic and copies ran while one was open for 16% -> 27% of each run, Pallas kernels for 53% -> 64%
where the time goes in v4:
time: 457 us; the launch traced here: 451 us
  Pallas kernels  287 us (63%)
  matrix products  93.7 us (21%)
  other arithmetic  35.2 us (8%)
  local copies, waits for them, and re-layouts  15.2 us (3%)
  between operations  15 us (3%)
    pallas_call x1, Pallas kernels, reduce_gradients(): pl.pallas_call(functools.partial(back_kernel, sp_size), out_shape=[jax.Sh...  144 us
    pallas_call x1, Pallas kernels, gather_weights(): pl.pallas_call(functools.partial(gather_kernel, sp_size), out_shape=[jax....  121 us
    dot_general x4, matrix products, contract_cols(): lax.dot_general(left, right, (((1,), (1,)), ((), ())), preferred_element_...  52.7 us
    dot_general x1, matrix products, body(): grad_mlp_in = jnp.dot(grad_pre, up_own, preferred_element_type=full)  14.8 us
    dot_general x1, matrix products, body(): jnp.dot(hidden, down_own, preferred_element_type=full)  13.1 us
    pallas_call x1, Pallas kernels, attend_bwd(): pl.pallas_call(functools.partial(bwd_kernel, HEAD ** (-0.5), heads), grid...  12.6 us
    pallas_call x1, Pallas kernels, attend_fwd(): pl.pallas_call(functools.partial(fwd_kernel, HEAD ** (-0.5)), grid_spec=p...  9.28 us
  transfers between devices with their start and end apart: 4, of which 1 were waited for; matrix products, arithmetic and copies ran while one was open for 27% of the time, Pallas kernels for 64%

profile of v4, /device:TPU:8, one launch (start us, length us, event | category | flops | bytes accessed | tf_op | source)
XLA Modules:
  0.0 450.6 jit_solution(12695016149463601679)
XLA Ops:
  7.2 0.0 all-gather.3.cloned.1.call-start
  7.2 0.7 all-gather.3.cloned.1.call-update
  7.9 0.0 all-gather.5.cloned.1.call-start
  8.0 0.7 all-gather.5.cloned.1.call-update
  8.7 0.0 reduce-scatter.3.cloned.1.call-start
  8.7 0.8 fusion.16
  9.5 0.8 fusion.17
  10.3 0.7 convert_bitcast_fusion
  11.0 0.6 copy.30
  11.6 0.1 pad.6.clone
  11.7 0.1 pad.9.clone
  12.4 0.7 reshape.133
  13.2 1.9 fusion.12
  15.1 121.1 %gather_weights.1 = (bf16[2048,1536]{1,0:T(8,128)(2,1)}, bf16[512,2048]{1,0:T(8,128)(2,1)}, bf16[2048,2048]{1,0:T(8,128)(2,1)}, bf16[2048,2048]{1,0:T(8,128)(2,1)}) custom-call(bf16[64,6144]{1,0:T(8,128)(2,1)} %qkv_ref.1, bf16[64,2048]{1,0:T(8,128)(2,1)} %out_ref.1, bf16[256,2048]{1,0:T(8,128)(2,1)} %up_ref.1, bf16[256,2048]{1,0:T(8,128)(2,1)} %down_ref.1), custom_call_target="tpu_custom_call" | custom-call | bytes 300000000 | tf_op jit(solution)/shard_map/gather_weights/pallas_call | solution.py:304
  136.2 1.3 maximum_maximum_fusion
  137.6 3.0 convert_reduce_fusion
  140.5 3.6 fusion.2
  144.2 4.4 add_convert_fusion.2
  148.7 8.7 %fusion.18.pq.pk.pv = f32[1024,1536]{1,0:T(8,128)} fusion(bf16[1024,2048]{1,0:T(8,128)(2,1)S(1)} %get-tuple-element.61.attn_hbm, bf16[2048,1536]{1,0:T(8,128)(2,1)S(1)} %bitcast.59), kind=kOutput, calls=%fused_computation.60 | convolution fusion | flops 6442450944 | bytes 16777216 | tf_op jit(solution)/shard_map/dot_general | solution.py:766
  157.4 9.3 %attend_fwd.1 = (bf16[1024,512]{1,0:T(8,128)(2,1)}, bf16[1024,512]{1,0:T(8,128)(2,1)}, bf16[1024,512]{1,0:T(8,128)(2,1)}, bf16[1024,512]{1,0:T(8,128)(2,1)}) custom-call(s32[1]{0:T(128)} %copy.37.len_ref, f32[1024,1536]{1,0:T(8,128)} %fusion.18.pq.pk.pv, f32[1024,1536]{1,0:T(8,128)} %fusion.18.pq.pk.pv, f32[1024,1536]{1,0:T(8,128)} %fusion.18.pq.pk.pv, ...), custom_call_target="tpu_custom_call" | custom-call | flops 2147483648 | bytes 12582912 | tf_op jit(solution)/shard_map/attend_fwd/pallas_call | solution.py:79
  166.7 15.2 %multiply_convert_fusion = (bf16[1024,2048]{1,0:T(8,128)(2,1)S(1)}, f32[1024,2048]{1,0:T(8,128)}) fusion(f32[2048]{0:T(1024)S(1)} %bitcast.49, bf16[1024,2048]{1,0:T(8,128)(2,1)} %get-tuple-element.62.mlp_hbm, bf16[2048,2048]{1,0:T(8,128)(2,1)} %get-tuple-element.35), kind=kOutput, calls=%fused_computation.15 | convolution fusion | flops 8602517504 | bytes 25174016 | tf_op jit(solution)/shard_map/dot_general | solution.py:29
  181.9 13.1 %fusion.19 = f32[1024,2048]{1,0:T(8,128)S(1)} fusion(bf16[1024,2048]{1,0:T(8,128)(2,1)S(1)} %get-tuple-element.72.hidden_hbm, bf16[2048,2048]{1,0:T(8,128)(2,1)} %get-tuple-element.36), kind=kOutput, calls=%fused_computation.61 | convolution fusion | flops 8589934592 | bytes 20971520 | tf_op jit(solution)/shard_map/dot_general | solution.py:773
  195.0 4.4 convolution_add_fusion
  199.4 0.0 reduce-scatter.3.cloned.1.call-update
  199.5 0.0 reduce-scatter.5.cloned.1.call-start
  199.5 0.0 all-gather.5.cloned.1.call-done
  199.5 2.5 broadcast_select_fusion.cot_hbm
  202.1 2.0 copy-done.2
  204.1 5.0 %convolution_convert_fusion.g_ref = bf16[1024,512]{1,0:T(8,128)(2,1)} fusion(bf16[1024,2048]{1,0:T(8,128)(2,1)S(1)} %broadcast_select_fusion.cot_hbm, bf16[512,2048]{1,0:T(8,128)(2,1)} %get-tuple-element.38), kind=kOutput, calls=%fused_computation.31 | convolution fusion | flops 2148007936 | bytes 7340032 | tf_op jit(solution)/shard_map/dot_general | solution.py:29
  209.0 12.6 %attend_bwd.1 = (bf16[1024,1536]{1,0:T(8,128)(2,1)}, f32[1,1536]{1,0:T(1,128)}) custom-call(s32[1]{0:T(128)} %copy.37.len_ref, bf16[1024,512]{1,0:T(8,128)(2,1)} %get-tuple-element.32.q_ref, bf16[1024,512]{1,0:T(8,128)(2,1)} %get-tuple-element.33.k_ref, bf16[1024,512]{1,0:T(8,128)(2,1)} %get-tuple-element.34.v_ref, ...), custom_call_target="tpu_custom_call" | custom-call | flops 5368709120 | bytes 10485760 | tf_op jit(solution)/shard_map/attend_bwd/pallas_call | solution.py:117
  221.6 16.4 %convert_reduce_fusion.1 = (f32[2048]{0:T(1024)S(1)}, bf16[1024,2048]{1,0:T(8,128)(2,1)S(1)}) fusion(f32[1024,2048]{1,0:T(8,128)} %get-tuple-element.73, f32[2048]{0:T(1024)S(1)} %bitcast.50, bf16[1024,2048]{1,0:T(8,128)(2,1)} %copy-done.2, bf16[2048,2048]{1,0:T(8,128)(2,1)} %get-tuple-element.36), kind=kOutput, calls=%fused_computation.12 | convolution fusion | flops 8617195520 | bytes 25182208 | tf_op jit(solution)/shard_map/dot_general | solution.py:29
  238.0 14.8 %fusion.20 = f32[1024,2048]{1,0:T(8,128)} fusion(bf16[1024,2048]{1,0:T(8,128)(2,1)S(1)} %get-tuple-element.75.pre_hbm, bf16[2048,2048]{1,0:T(8,128)(2,1)} %get-tuple-element.35), kind=kOutput, calls=%fused_computation.62 | convolution fusion | flops 8589934592 | bytes 20971520 | tf_op jit(solution)/shard_map/dot_general | solution.py:783
  252.8 0.0 copy-start.9
  252.8 16.1 %fusion.13 = (f32[2048]{0:T(1024)S(1)}, f32[2048]{0:T(1024)S(1)}, bf16[1024,2048]{1,0:T(8,128)(2,1)}, f32[2048]{0:T(1024)S(1)}, f32[2048]{0:T(1024)S(1)}, /*index=5*/f32[1024,2048]{1,0:T(8,128)}) fusion(f32[1024]{0:T(1024)S(1)} %add_rsqrt_fusion, f32[1024]{0:T(1024)S(1)} %broadcast_multiply_fusion, bf16[1024,2048]{1,0:T(8,128)(2,1)S(1)} %copy-done.1, ...), kind=kOutput, calls=%fused_computation.55 | convolution fusion | flops 6469705728 | bytes 34660352 | tf_op jit(solution)/shard_map/dot_general | solution.py:29
  269.0 0.0 reduce-scatter.5.cloned.1.call-update
  269.0 0.6 convert_element_type.120
  269.7 0.1 dynamic_update_slice.8
  269.8 0.1 dynamic_update_slice.9
  269.9 0.7 dynamic-slice.3
  270.6 1.4 convert_reduce_fusion.3
  272.0 0.6 constant_dynamic-update-slice_fusion.4
  272.6 0.6 constant_dynamic-update-slice_fusion.3
  273.2 0.6 constant_dynamic-update-slice_fusion.2
  273.8 0.6 constant_dynamic-update-slice_fusion.1
  274.4 0.6 constant_dynamic-update-slice_fusion.small_ref
  275.0 2.8 reduce-scatter.3.cloned.1.call-done
  277.9 144.0 %reduce_gradients.1 = (bf16[256,2048]{1,0:T(8,128)(2,1)}, bf16[256,2048]{1,0:T(8,128)(2,1)}, bf16[64,6144]{1,0:T(8,128)(2,1)}, bf16[64,2048]{1,0:T(8,128)(2,1)}, f32[192,128]{1,0:T(8,128)}) custom-call(bf16[1024,2048]{1,0:T(8,128)(2,1)} %copy-done.14, bf16[1024,2048]{1,0:T(8,128)(2,1)} %copy-done.2, bf16[1024,2048]{1,0:T(8,128)(2,1)} %copy-done.15, ...), custom_call_target="tpu_custom_call" | custom-call | flops 25999998976 | bytes 300000000 | tf_op jit(solution)/shard_map/reduce_gradients/pallas_call | solution.py:646
  421.9 0.0 copy-start.3
  421.9 0.0 copy-start.8
  421.9 0.0 reduce-scatter.5.cloned.1.call-done
  422.0 0.9 split.21
  422.9 0.8 fusion.15
  423.7 1.4 slice_bitcast_fusion
  425.1 1.3 slice_bitcast_fusion.1
  426.4 2.8 convert_element_type.127
  429.1 2.8 convert_element_type.128
  431.9 2.4 convert_element_type.125
  434.3 2.1 convert_reduce_fusion.2
  436.4 0.8 convert_element_type.126
  437.3 0.6 reshape.139
  437.9 0.6 reshape.137
  438.5 0.6 reshape.138
  439.1 1.4 add_convert_fusion.3
  440.5 3.4 fusion.8
  (52 shorter events, 0.2 us)
Async XLA Ops:
  7.2 130.4 %all-gather.3.cloned.1.call-start = ((), (), s32[]{:S(2)}) async-start(), calls=%async_computation.2 | async-start | bytes 5242880 | tf_op jit(solution)/shard_map/all_gather | solution.py:736
  7.9 191.6 %all-gather.5.cloned.1.call-start = ((), (), s32[]{:S(2)}) async-start(), calls=%async_computation.3 | async-start | bytes 5242880 | tf_op jit(solution)/shard_map/all_gather | solution.py:737
  8.7 269.2 %reduce-scatter.3.cloned.1.call-start = ((), (), s32[]{:S(2)}) async-start(), calls=%async_computation.4 | async-start | bytes 5242880 | tf_op jit(solution)/shard_map/reduce_scatter | solution.py:776
  137.6 6.6 %copy-start = (bf16[1024,2048]{1,0:T(8,128)(2,1)S(1)}, bf16[1024,2048]{1,0:T(8,128)(2,1)}, u32[]{:S(2)}) copy-start(bf16[1024,2048]{1,0:T(8,128)(2,1)} %all-gather.3.cloned.1.call-done) | copy-start | bytes 12582916
  140.5 8.1 %slice-start = ((s8[6291456]{0:T(1024)(128)(4,1)}), s8[4194304]{0:T(1024)(128)(4,1)S(1)}, s32[]{:S(2)}) async-start(s8[6291456]{0:T(1024)(128)(4,1)} %bitcast.58), calls=%async_computation.6 | async-start | bytes 8388608
  144.2 4.5 slice-start.1
  148.6 8.7 %copy-start.5 = (bf16[1024,2048]{1,0:T(8,128)(2,1)}, bf16[1024,2048]{1,0:T(8,128)(2,1)S(1)}, u32[]{:S(2)}) copy-start(bf16[1024,2048]{1,0:T(8,128)(2,1)S(1)} %get-tuple-element.61.attn_hbm) | copy-start | bytes 12582916
  181.9 13.1 %copy-start.14 = (bf16[1024,2048]{1,0:T(8,128)(2,1)}, bf16[1024,2048]{1,0:T(8,128)(2,1)S(1)}, u32[]{:S(2)}) copy-start(bf16[1024,2048]{1,0:T(8,128)(2,1)S(1)} %get-tuple-element.72.hidden_hbm) | copy-start | bytes 12582916
  181.9 13.1 %copy-start.12 = (bf16[512,2048]{1,0:T(8,128)(2,1)S(1)}, bf16[512,2048]{1,0:T(8,128)(2,1)}, u32[]{:S(2)}) copy-start(bf16[512,2048]{1,0:T(8,128)(2,1)} %get-tuple-element.38) | copy-start | bytes 6291460
  181.9 13.1 %copy-start.13 = (bf16[1024,512]{1,0:T(8,128)(2,1)S(1)}, bf16[1024,512]{1,0:T(8,128)(2,1)}, u32[]{:S(2)}) copy-start(bf16[1024,512]{1,0:T(8,128)(2,1)} %get-tuple-element.37.ctx_hbm) | copy-start | bytes 3145732
  199.5 222.5 %reduce-scatter.5.cloned.1.call-start = ((), (), s32[]{:S(2)}) async-start(), calls=%async_computation.5 | async-start | bytes 5242880 | tf_op jit(solution)/shard_map/reduce_scatter | solution.py:791
  202.1 2.0 copy-start.2
  237.9 14.9 %copy-start.15 = (bf16[1024,2048]{1,0:T(8,128)(2,1)}, bf16[1024,2048]{1,0:T(8,128)(2,1)S(1)}, u32[]{:S(2)}) copy-start(bf16[1024,2048]{1,0:T(8,128)(2,1)S(1)} %get-tuple-element.75.pre_hbm) | copy-start | bytes 12582916
  238.0 14.9 %copy-start.1 = (bf16[1024,2048]{1,0:T(8,128)(2,1)S(1)}, bf16[1024,2048]{1,0:T(8,128)(2,1)}, u32[]{:S(2)}) copy-start(bf16[1024,2048]{1,0:T(8,128)(2,1)} %all-gather.3.cloned.1.call-done) | copy-start | bytes 12582916
  252.8 16.2 %copy-start.10 = (bf16[2048]{0:T(1024)(128)(2,1)S(1)}, bf16[2048]{0:T(1024)(128)(2,1)}, u32[]{:S(2)}) copy-start(bf16[2048]{0:T(1024)(128)(2,1)} %param.23) | copy-start | bytes 12292
  252.8 16.9 %copy-start.9 = (f32[1,1536]{1,0:T(1,128)S(1)}, f32[1,1536]{1,0:T(1,128)}, u32[]{:S(2)}) copy-start(f32[1,1536]{1,0:T(1,128)} %get-tuple-element.41) | copy-start | bytes 18436
  421.9 14.5 %copy-start.7 = (bf16[64,2048]{1,0:T(8,128)(2,1)S(1)}, bf16[64,2048]{1,0:T(8,128)(2,1)}, u32[]{:S(2)}) copy-start(bf16[64,2048]{1,0:T(8,128)(2,1)} %get-tuple-element.48) | copy-start | bytes 786436
  421.9 17.2 %copy-start.3 = (bf16[256,2048]{1,0:T(8,128)(2,1)S(1)}, bf16[256,2048]{1,0:T(8,128)(2,1)}, u32[]{:S(2)}) copy-start(bf16[256,2048]{1,0:T(8,128)(2,1)} %param.12) | copy-start | bytes 3145732
  421.9 17.2 %copy-start.6 = (bf16[256,2048]{1,0:T(8,128)(2,1)S(1)}, bf16[256,2048]{1,0:T(8,128)(2,1)}, u32[]{:S(2)}) copy-start(bf16[256,2048]{1,0:T(8,128)(2,1)} %reduce-scatter.3.cloned.1.call-done) | copy-start | bytes 3145732
  421.9 17.2 %copy-start.8 = (f32[2048]{0:T(1024)S(1)}, f32[2048]{0:T(1024)}, u32[]{:S(2)}) copy-start(f32[2048]{0:T(1024)} %convert_element_type.120) | copy-start | bytes 24580
  421.9 18.6 %copy-start.11 = (f32[256]{0:T(256)S(1)}, f32[256]{0:T(256)}, u32[]{:S(2)}) copy-start(f32[256]{0:T(256)} %dynamic-slice.3) | copy-start | bytes 3076
  422.0 12.3 %copy-start.4 = (bf16[256,2048]{1,0:T(8,128)(2,1)S(1)}, bf16[256,2048]{1,0:T(8,128)(2,1)}, u32[]{:S(2)}) copy-start(bf16[256,2048]{1,0:T(8,128)(2,1)} %reduce-scatter.5.cloned.1.call-done) | copy-start | bytes 3145732
Sparse Core Ops, SparseCore 0:
  9.6 106.9 all-gather.2
  118.2 79.3 all-gather.4
  199.9 77.9 reduce-scatter.2
  280.1 97.9 reduce-scatter.4
